TPU v7x, 32 devices: a whole 2x2x4 slice. The times are simulated.
32 devices in a mesh: gx: 4 (over z), gy: 8 (over y, x, core).
Axes of the slice: x: 2, y: 2, z: 4, core: 2. Of those that a mesh axis runs over, the one named last changes fastest.
Arguments:
- point_feats: bfloat16 [512, 64, 128], P(('gx', 'gy')), may hold values from -6 to 6
- offsets: bfloat16 [512, 3, 128], P(('gx', 'gy')), may hold values from 0 to 1
- targets: int32 [512, 1], P(('gx', 'gy')), may hold values from 0 to 7; in each aligned block of 16 rows (0 to 15, 16 to 31, ...) at most 4 rows name the same one
- zstart: int32 [512], P(('gx', 'gy')), may hold values from 0 to 63
- enc_in: float32 [3, 64], replicated, may hold values from -4 to 4
- enc_bias: float32 [64], replicated, may hold values from -4 to 4
- enc_out: bfloat16 [64, 64], replicated, may hold values from -0.75 to 0.75
- dec_in: float32 [3, 64], replicated, may hold values from -4 to 4
- dec_bias: float32 [64], replicated, may hold values from -4 to 4
- dec_out: bfloat16 [64, 64], replicated, may hold values from -0.75 to 0.75
- spec_weight: float32 [32, 32, 32, 4096], P(None, 'gx', 'gy'), may hold values from -0.75 to 0.75
- local_weight: float32 [64, 64], replicated, may hold values from -0.75 to 0.75
- local_bias: float32 [64], replicated, may hold values from -3 to 3
- head_weight: float32 [64], replicated, may hold values from -4 to 4
Outputs:
- pressure: float32 [512, 128], P(('gx', 'gy'))
Inputs may be any that keep to these rules, and one draw needn't show every extreme that they name: `targets`: A block's cells lie in the pencil of its own gx row with this gy index; at most 4 blocks of one device share a target, and exactly 4 do on some devices.
All inputs are finite; a program needn't handle non-finite values.
Results may differ from a plain program's by a relative error of at most 0.0014.
Values may be sent and summed in bfloat16 or wider, within the bound.
No kernel may reach another device: no remote copies, remote signals or barrier semaphores. Data moves between devices by JAX's collectives and lax.ppermute only.
A program may use at most 128 MiB of HBM per device.

v0:
```python
import jax
import jax.numpy as jnp
from jax import lax
from jax.sharding import PartitionSpec as P

G = 64
M = 32


kernel_spread = 2.0
highest = lax.Precision.HIGHEST


def real_basis(length, modes):
    half = modes // 2
    places = jnp.arange(length).astype(jnp.float32)
    frequency = jnp.arange(half).astype(jnp.float32)
    angle_cos = 2.0 * jnp.pi * frequency[:, None] * places[None, :] / length
    angle_sin = 2.0 * jnp.pi * (frequency[:, None] + 1.0) * places[None, :] / length
    table = jnp.concatenate([jnp.cos(angle_cos), jnp.sin(angle_sin)], 0)
    return table * jnp.float32((2.0 / length) ** 0.5)


def tile_terms(offset_rows, weight_in, bias_in, cells_x, cells_y):
    offset_rows = offset_rows.astype(jnp.float32)
    cell_ids = jnp.arange(cells_x * cells_y)
    center_x = (cell_ids // cells_y).astype(jnp.float32) + 0.5
    center_y = (cell_ids % cells_y).astype(jnp.float32) + 0.5
    delta_x = (center_x[None, :, None] - cells_x * offset_rows[:, 0][:, None, :]) / kernel_spread
    delta_y = (center_y[None, :, None] - cells_y * offset_rows[:, 1][:, None, :]) / kernel_spread
    delta_z = (0.5 - offset_rows[:, 2][:, None, :]) / kernel_spread
    closeness = jnp.exp(-0.5 * (delta_x * delta_x + delta_y * delta_y + delta_z * delta_z))
    before = (
        delta_x[..., None] * weight_in[0]
        + delta_y[..., None] * weight_in[1]
        + delta_z[..., None] * weight_in[2]
        + bias_in
    )
    return (jax.nn.gelu(before, approximate=False) * closeness[..., None]).astype(jnp.bfloat16)


def encode(weighted, feats, out_weight):
    partial_sums = jnp.einsum("bcph,bop->bcho", weighted, feats, preferred_element_type=jnp.float32)
    return jnp.einsum(
        "bcho,ho->boc", partial_sums, out_weight.astype(jnp.float32), precision=highest
    ) * feats.shape[2] ** (-0.5)


def decode(weighted, tile_values, out_weight):
    folded = (
        out_weight.astype(jnp.float32)[None, None, :, :]
        * jnp.transpose(tile_values.astype(jnp.float32), (0, 2, 1))[:, :, None, :]
    ).astype(jnp.bfloat16)
    return jnp.einsum(
        "bcph,bcho->bop", weighted, folded, preferred_element_type=jnp.float32
    ) * weighted.shape[1] ** (-0.5)


def run_groups(function, arrays, row_count):
    group_size = 8
    shaped = tuple(
        (
            member.reshape((row_count // group_size, group_size) + member.shape[1:])
            for member in arrays
        )
    )
    result = lax.map(function, shaped)
    return result.reshape((row_count,) + result.shape[2:])


def fourier(pencil, spec_weight, local_weight, local_bias, table):
    channels = pencil.shape[0]
    spectrum = jnp.einsum("oxyz,kz->oxyk", pencil, table, precision=highest)
    spectrum = lax.all_to_all(
        spectrum.astype(jnp.bfloat16), "gy", split_axis=3, concat_axis=2, tiled=True
    ).astype(spectrum.dtype)
    spectrum = jnp.einsum("oxyk,ly->oxlk", spectrum, table, precision=highest)
    spectrum = lax.all_to_all(spectrum, "gx", split_axis=2, concat_axis=1, tiled=True)
    spectrum = jnp.einsum("oxlk,jx->ojlk", spectrum, table, precision=highest)
    mode_weight = spec_weight.reshape(spec_weight.shape[:3] + (channels, channels))
    mixed_modes = jnp.einsum("ojlk,jlkoq->qjlk", spectrum, mode_weight, precision=highest)
    returned = jnp.einsum("ojlk,jx->oxlk", mixed_modes, table, precision=highest)
    returned = lax.all_to_all(
        returned.astype(jnp.bfloat16), "gx", split_axis=1, concat_axis=2, tiled=True
    ).astype(returned.dtype)
    returned = jnp.einsum("oxlk,ly->oxyk", returned, table, precision=highest)
    returned = lax.all_to_all(
        returned.astype(jnp.bfloat16), "gy", split_axis=2, concat_axis=3, tiled=True
    ).astype(returned.dtype)
    returned = jnp.einsum("oxyk,kz->oxyz", returned, table, precision=highest)
    local_term = (
        jnp.einsum("oxyz,oq->qxyz", pencil, local_weight, precision=highest)
        + local_bias[:, None, None, None]
    )
    return jax.nn.gelu(returned + local_term, approximate=False).astype(jnp.bfloat16)


def local(
    point_feats,
    offsets,
    targets,
    zstart,
    enc_in,
    enc_bias,
    enc_out,
    dec_in,
    dec_bias,
    dec_out,
    spec_weight,
    local_weight,
    local_bias,
    head_weight,
):
    rows_count = lax.axis_size("gx")
    cols_count = lax.axis_size("gy")
    cells_x = G // rows_count
    cells_y = G // cols_count
    tile_cells = cells_x * cells_y
    block_count = point_feats.shape[0]
    channels = point_feats.shape[1]
    capacity = max(2, 2 * block_count // cols_count)
    slot_count = cols_count * capacity
    target = targets[:, 0]
    onehot = (target[:, None] == jnp.arange(cols_count)[None, :]).astype(jnp.int32)
    slot_rank = jnp.sum(onehot * (jnp.cumsum(onehot, axis=0) - onehot), axis=1)
    slot_of = target * capacity + slot_rank
    placement = jnp.arange(slot_count)[:, None] == slot_of[None, :]
    place_float = placement.astype(jnp.float32)
    place_half = placement.astype(jnp.bfloat16)
    planes_sent = jnp.dot(place_float, zstart.astype(jnp.float32), precision=highest)
    table = real_basis(G, M)

    def encode_rows(pieces):
        feats_group, offs_group = pieces
        weighted = tile_terms(offs_group, enc_in, enc_bias, cells_x, cells_y)
        return encode(weighted, feats_group, enc_out)

    def decode_rows(pieces):
        tiles_group, offs_group = pieces
        weighted = tile_terms(offs_group, dec_in, dec_bias, cells_x, cells_y)
        values = decode(weighted, tiles_group, dec_out)
        return jnp.einsum(
            "bop,o->bp", jax.nn.gelu(values, approximate=False), head_weight, precision=highest
        )

    own_terms = run_groups(encode_rows, (point_feats, offsets), block_count)
    send_terms = jnp.einsum("sb,boc->soc", place_float, own_terms, precision=highest)
    got_terms, got_planes = (
        lax.all_to_all(
            send_terms.reshape(cols_count, capacity, channels, tile_cells),
            "gy",
            split_axis=0,
            concat_axis=0,
            tiled=True,
        ),
        lax.all_to_all(
            planes_sent.reshape(cols_count, capacity), "gy", split_axis=0, concat_axis=0, tiled=True
        ),
    )
    contrib = got_terms.reshape(slot_count, channels, tile_cells)
    planes_got = got_planes.reshape(slot_count)
    plane_table = planes_got[:, None] == jnp.arange(G).astype(jnp.float32)[None, :]
    pencil = jnp.einsum("soc,sz->ocz", contrib, plane_table.astype(jnp.float32), precision=highest)
    pencil = pencil.reshape(channels, cells_x, cells_y, G)
    latent = fourier(pencil, spec_weight, local_weight, local_bias, table).reshape(
        channels, tile_cells, G
    )
    tile_values = jnp.einsum(
        "ocz,sz->soc", latent, plane_table.astype(jnp.bfloat16), preferred_element_type=jnp.float32
    ).astype(jnp.bfloat16)
    returned = lax.all_to_all(
        tile_values.reshape(cols_count, capacity, channels, tile_cells),
        "gy",
        split_axis=0,
        concat_axis=0,
        tiled=True,
    )
    returned = returned.reshape(slot_count, channels, tile_cells)
    own_tiles = jnp.einsum(
        "sb,soc->boc", place_half, returned, preferred_element_type=jnp.float32
    ).astype(jnp.bfloat16)
    return run_groups(decode_rows, (own_tiles, offsets), block_count)


def solution(mesh):
    placed = (
        P(("gx", "gy"), None, None),
        P(("gx", "gy"), None, None),
        P(("gx", "gy"), None),
        P(("gx", "gy")),
        P(),
        P(),
        P(),
        P(),
        P(),
        P(),
        P(None, "gx", "gy", None),
        P(),
        P(),
        P(),
    )
    return jax.shard_map(
        local, mesh=mesh, in_specs=placed, out_specs=P(("gx", "gy"), None), check_vma=False
    )
```

profile of v0, /device:TPU:0, one launch (start us, length us, event | category | flops | bytes accessed | tf_op | source)
XLA Modules:
  0.0 560.5 jit_solution(12473694886595939378)
XLA Ops:
  0.8 0.8 select_reduce_fusion
  2.8 0.8 convolution_bitcast_fusion.2
  4.4 5.2 all-to-all-start
  10.1 1.3 copy.59
  11.5 179.2 %while.24 = (s32[]{:T(128)}, f32[2,8,64,128]{3,2,1,0:T(8,128)}, bf16[2,8,3,128]{3,1,2,0:T(8,128)(2,1)}, f32[3,64]{1,0:T(4,128)}, f32[64]{0:T(128)}, /*index=5*/b...) while((s32[]{:T(128)}, f32[2,8,64,128]{3,2,1,0:T(8,128)}, bf16[2,8,3,128]{3,1,2,0:T(8,128)(2,1)}, ...), condition=%wide.region_3.4_spmd, body=%wide.region_2.3_spmd.sunk | while | flops 1678981120 | bytes 9416085 | solution.py:67
  12.5 0.8 slice_bitcast_fusion.8
  14.1 85.9 %multiply_reduce_fusion.2 = f32[64,8,128]{0,2,1:T(8,128)S(1)} fusion(f32[64,64]{0,1:T(8,128)S(1)} %bitcast_convert_fusion.6, f32[8,128,128]{2,1,0:T(8,128)S(1)} %get-tuple-element.435, f32[64]{0:T(128)} %get-tuple-element.482, f32[8,128,64]{1,2,0:T(8,128)S(1)} %broadcast_multiply_fusion.4, f32[64]{0:T(128)S(1)} %get-tuple-element.438, ...), kind=kOutput, calls=%fused_computation.219.clone.3 | convolution fusion | flops 1677656064 | bytes 2246144 | tf_op jit(solution)/shard_map/while/body/eval_jaxpr/bcph,bop->bcho/dot_general | solution.py:43
  102.0 0.8 slice_bitcast_fusion.8
  103.6 85.9 %multiply_reduce_fusion.2 = f32[64,8,128]{0,2,1:T(8,128)S(1)} fusion(f32[64,64]{0,1:T(8,128)S(1)} %bitcast_convert_fusion.6, f32[8,128,128]{2,1,0:T(8,128)S(1)} %get-tuple-element.435, f32[64]{0:T(128)} %get-tuple-element.482, f32[8,128,64]{1,2,0:T(8,128)S(1)} %broadcast_multiply_fusion.4, f32[64]{0:T(128)S(1)} %get-tuple-element.438, ...), kind=kOutput, calls=%fused_computation.219.clone.3 | convolution fusion | flops 1677656064 | bytes 2246144 | tf_op jit(solution)/shard_map/while/body/eval_jaxpr/bcph,bop->bcho/dot_general | solution.py:43
  190.7 1.8 fusion.300
  192.6 1.2 copy.61
  193.8 4.2 all-to-all-start.1
  198.6 1.3 reduce.5
  200.0 13.3 %all-to-all-done.1 = f32[8,4,64,128]{3,2,1,0:T(8,128)S(1)} async-done(((f32[8,4,64,128]{3,2,1,0:T(8,128)}), f32[8,4,64,128]{3,2,1,0:T(8,128)S(1)}, u32[]{:S(2)}, u32[]{:S(2)}) %all-to-all-start.1) | async-done | bytes 1048608 | tf_op jit(solution)/shard_map/all_to_all | solution.py:149
  213.3 1.8 copy.62
  215.2 3.5 fusion.309
  218.7 2.1 copy-done.1
  220.8 11.4 %convolution_convert_fusion.1 = bf16[64,16,8,32]{0,3,2,1:T(8,128)(2,1)S(1)} fusion(f32[64,16,8,64]{3,0,2,1:T(8,128)S(1)} %fusion.309, f32[16,64]{1,0:T(8,128)S(1)} %get-tuple-element.319, f32[16,64]{1,0:T(8,128)S(1)} %get-tuple-element.318), kind=kOutput, calls=%fused_computation.359 | convolution fusion | flops 201592832 | bytes 2629632 | tf_op jit(solution)/shard_map/oxyz,kz->oxyk/dot_general | solution.py:73
  232.6 1.1 reshape.239
  233.8 12.1 %all_to_all.91 = bf16[8,2,16384]{2,1,0:T(2,128)(2,1)S(1)} all-to-all(bf16[8,2,16384]{2,1,0:T(2,128)(2,1)S(1)} %reshape.239), channel_id=1, replica_groups=mesh['gx'=4,'gy'=8] {'gy'}, dimensions={0} | all-to-all | bytes 1048576 | tf_op jit(solution)/shard_map/all_to_all | solution.py:74
  247.8 1.8 reshape.241
  249.6 4.9 all-to-all-start.3
  254.5 28.9 %reshape.204 = f32[32,8,4,64,64]{4,3,2,1,0:T(8,128)} reshape(f32[32,8,4,4096]{3,2,1,0:T(4,128)} %param.28) | data formatting | bytes 33554432 | tf_op jit(solution)/shard_map/reshape | solution.py:80
  283.9 2.1 reduce.8
  287.5 1.2 convolution_bitcast_fusion.1
  288.8 32.4 %fusion.303 = f32[32,8,4,1,64]{4,3,2,1,0:T(1,128)S(1)} fusion(f32[32,8,4,64,64]{4,3,2,1,0:T(8,128)} %reshape.204, f32[64,32,8,4,1]{0,1,3,2,4:T(8,128)S(1)} %convolution_bitcast_fusion.1), kind=kOutput, calls=%fused_computation.378 | convolution fusion | flops 50331648 | bytes 17301504 | tf_op jit(solution)/shard_map/ojlk,jlkoq->qjlk/dot_general | solution.py:81
  321.2 1.2 fusion.293
  323.3 12.7 %all_to_all.92 = bf16[4,2,16384]{2,1,0:T(2,128)(2,1)S(1)} all-to-all(bf16[4,2,16384]{2,1,0:T(2,128)(2,1)S(1)} %reshape.243), channel_id=1, replica_groups=mesh['gx'=4,'gy'=8] {'gx'}, dimensions={0} | all-to-all | bytes 524288 | tf_op jit(solution)/shard_map/all_to_all | solution.py:83
  336.3 1.0 fusion.289
  337.4 0.8 copy.138
  338.9 12.5 %all_to_all.93 = bf16[8,2,16384]{2,1,0:T(2,128)(2,1)S(1)} all-to-all(bf16[8,2,16384]{2,1,0:T(2,128)(2,1)S(1)} %reshape.245), channel_id=1, replica_groups=mesh['gx'=4,'gy'=8] {'gy'}, dimensions={0} | all-to-all | bytes 1048576 | tf_op jit(solution)/shard_map/all_to_all | solution.py:87
  352.6 2.4 fusion.323
  355.0 14.5 %fusion.279 = bf16[64,16,8,64]{3,0,2,1:T(8,128)(2,1)S(1)} fusion(f32[64,16,8,64]{3,0,2,1:T(8,128)S(1)} %fusion.323, f32[64,16,8,64]{3,0,2,1:T(8,128)} %copy-done.1, f32[64]{0:T(128)S(1)} %copy-done.11, f32[64,64]{1,0:T(8,128)S(1)} %copy-done), kind=kOutput, calls=%fused_computation.339 | convolution fusion | flops 437780480 | bytes 5259520 | tf_op jit(solution)/shard_map/oxyz,oq->qxyz/dot_general | solution.py:92
  369.5 1.4 fusion.290
  370.9 1.0 copy.78
  371.9 3.5 all-to-all-start.6
  375.4 9.6 %all-to-all-done.6 = bf16[8,4,64,128]{3,1,2,0:T(4,128)(2,1)S(1)} async-done(((bf16[8,4,64,128]{3,1,2,0:T(4,128)(2,1)}), bf16[8,4,64,128]{3,1,2,0:T(4,128)(2,1)S(1)}, u32[]{:S(2)}, u32[]{:S(2)}) %all-to-all-start.6) | async-done | bytes 524320 | tf_op jit(solution)/shard_map/all_to_all | solution.py:171
  385.3 1.0 fusion.294
  386.2 174.1 %while.25 = (s32[]{:T(128)}, f32[2,8,128]{2,1,0:T(8,128)}, bf16[64,64]{1,0:T(8,128)(2,1)S(1)}, bf16[2,8,64,128]{3,1,0,2:T(8,128)(2,1)}, bf16[2,8,3,128]{3,1,2,0:...) while((s32[]{:T(128)}, f32[2,8,128]{2,1,0:T(8,128)}, ...), condition=%wide.region_5.6_spmd, body=%wide.region_4.5_spmd.sunk | while | flops 1684092928 | bytes 22110176 | solution.py:67
  387.4 0.8 slice_bitcast_fusion.9
  388.3 0.9 constant_dynamic-slice_fusion.2
  389.3 2.2 multiply_convert_fusion.9
  391.5 80.4 %fusion.380 = f32[8,64,128]{2,1,0:T(8,128)S(1)} fusion(f32[8,128,128]{2,1,0:T(8,128)S(1)} %get-tuple-element.455, f32[64]{0:T(128)S(1)} %get-tuple-element.510, f32[8,128,64]{1,2,0:T(8,128)S(1)} %broadcast_multiply_fusion.5, f32[64]{0:T(128)S(1)} %get-tuple-element.458, f32[8,128,128]{2,1,0:T(8,128)S(1)} %get-tuple-element.459, ...), kind=kOutput, calls=%fused_computation.27.clone.3 | convolution fusion | flops 1669332992 | bytes 10486528 | tf_op jit(solution)/shard_map/while/body/eval_jaxpr/bcph,bcho->bop/dot_general | solution.py:54
  471.9 0.8 fusion.381
  475.2 0.9 constant_dynamic-slice_fusion.2
  476.2 2.2 multiply_convert_fusion.9
  478.5 80.4 %fusion.380 = f32[8,64,128]{2,1,0:T(8,128)S(1)} fusion(f32[8,128,128]{2,1,0:T(8,128)S(1)} %get-tuple-element.455, f32[64]{0:T(128)S(1)} %get-tuple-element.510, f32[8,128,64]{1,2,0:T(8,128)S(1)} %broadcast_multiply_fusion.5, f32[64]{0:T(128)S(1)} %get-tuple-element.458, f32[8,128,128]{2,1,0:T(8,128)S(1)} %get-tuple-element.459, ...), kind=kOutput, calls=%fused_computation.27.clone.3 | convolution fusion | flops 1669332992 | bytes 10486528 | tf_op jit(solution)/shard_map/while/body/eval_jaxpr/bcph,bcho->bop/dot_general | solution.py:54
  558.9 0.8 fusion.381
  (101 shorter events, 21.3 us)
Async XLA Ops:
  0.0 355.0 %copy-start = (f32[64,64]{1,0:T(8,128)S(1)}, f32[64,64]{1,0:T(8,128)}, u32[]{:S(2)}) copy-start(f32[64,64]{1,0:T(8,128)} %param.29) | copy-start | bytes 49156
  2.3 0.6 copy-start.7
  4.4 189.4 %all-to-all-start = ((f32[8,1,4]{2,1,0:T(1,128)}), f32[8,1,4]{2,1,0:T(1,128)}, u32[]{:S(2)}, u32[]{:S(2)}) async-start(f32[8,1,4]{2,1,0:T(1,128)} %bitcast.37), calls=%async_computation | async-start | bytes 8192 | tf_op jit(solution)/shard_map/all_to_all | solution.py:156
  11.5 179.3 %copy-start.6 = (s32[8,4]{0,1:T(4,128)S(1)}, s32[8,4]{0,1:T(4,128)}, u32[]{:S(2)}) copy-start(s32[8,4]{0,1:T(4,128)} %multiply_add_fusion) | copy-start | bytes 388
  11.5 179.3 %copy-start.8 = (s32[16]{0:T(128)S(1)}, s32[16]{0:T(128)}, u32[]{:S(2)}) copy-start(s32[16]{0:T(128)} %copy-done.7) | copy-start | bytes 196
  14.1 86.1 %copy-start.2 = (f32[2,8,64,128]{3,2,1,0:T(8,128)S(1)}, f32[2,8,64,128]{3,2,1,0:T(8,128)}, u32[]{:S(2)}) copy-start(f32[2,8,64,128]{3,2,1,0:T(8,128)} %get-tuple-element.471) | copy-start | bytes 1572868 | tf_op jit(solution)/shard_map/while
  100.2 0.8 copy-start.3
  103.6 86.1 %copy-start.2 = (f32[2,8,64,128]{3,2,1,0:T(8,128)S(1)}, f32[2,8,64,128]{3,2,1,0:T(8,128)}, u32[]{:S(2)}) copy-start(f32[2,8,64,128]{3,2,1,0:T(8,128)} %get-tuple-element.471) | copy-start | bytes 1572868 | tf_op jit(solution)/shard_map/while
  189.7 0.8 copy-start.3
  193.8 19.6 %all-to-all-start.1 = ((f32[8,4,64,128]{3,2,1,0:T(8,128)}), f32[8,4,64,128]{3,2,1,0:T(8,128)S(1)}, u32[]{:S(2)}, u32[]{:S(2)}) async-start(f32[8,4,64,128]{3,2,1,0:T(8,128)} %copy.61), calls=%async_computation.1 | async-start | bytes 2097152 | tf_op jit(solution)/shard_map/all_to_all | solution.py:149
  218.7 2.1 copy-start.1
  249.6 33.8 %all-to-all-start.3 = ((f32[4,1,32768]{2,1,0:T(1,128)}), f32[4,1,32768]{2,1,0:T(1,128)S(1)}, u32[]{:S(2)}, u32[]{:S(2)}) async-start(f32[4,1,32768]{2,1,0:T(1,128)} %reshape.241), calls=%async_computation.3 | async-start | bytes 1048576 | tf_op jit(solution)/shard_map/all_to_all | solution.py:78
  287.4 67.6 %copy-start.11 = (f32[64]{0:T(128)S(1)}, f32[64]{0:T(128)}, u32[]{:S(2)}) copy-start(f32[64]{0:T(128)} %param.30) | copy-start | bytes 772
  355.0 31.3 %copy-start.4 = (bf16[64,64]{1,0:T(8,128)(2,1)S(1)}, bf16[64,64]{1,0:T(8,128)(2,1)}, u32[]{:S(2)}) copy-start(bf16[64,64]{1,0:T(8,128)(2,1)} %param.27) | copy-start | bytes 24580
  355.0 31.3 %copy-start.12 = (f32[64]{0:T(128)S(1)}, f32[64]{0:T(128)}, u32[]{:S(2)}) copy-start(f32[64]{0:T(128)} %param.26) | copy-start | bytes 772
  371.9 13.1 %all-to-all-start.6 = ((bf16[8,4,64,128]{3,1,2,0:T(4,128)(2,1)}), bf16[8,4,64,128]{3,1,2,0:T(4,128)(2,1)S(1)}, u32[]{:S(2)}, u32[]{:S(2)}) async-start(bf16[8,4,64,128]{3,1,2,0:T(4,128)(2,1)} %copy.78), calls=%async_computation.6 | async-start | bytes 1048576 | tf_op jit(solution)/shard_map/all_to_all | solution.py:171
  391.5 80.4 %copy-start.13 = (f32[64]{0:T(128)S(1)}, f32[64]{0:T(128)}, u32[]{:S(2)}) copy-start(f32[64]{0:T(128)} %get-tuple-element.511) | copy-start | bytes 772 | tf_op jit(solution)/shard_map/while
  391.5 81.2 %copy-start.9 = (f32[2,8,128]{2,1,0:T(8,128)S(1)}, f32[2,8,128]{2,1,0:T(8,128)}, u32[]{:S(2)}) copy-start(f32[2,8,128]{2,1,0:T(8,128)} %get-tuple-element.496) | copy-start | bytes 24580 | tf_op jit(solution)/shard_map/while
  391.5 81.8 %copy-start.5 = (bf16[64,64]{1,0:T(8,128)(2,1)S(1)}, bf16[64,64]{1,0:T(8,128)(2,1)}, u32[]{:S(2)}) copy-start(bf16[64,64]{1,0:T(8,128)(2,1)} %get-tuple-element.525) | copy-start | bytes 24580 | tf_op jit(solution)/shard_map/while
  472.7 0.6 copy-start.10
  478.4 80.4 %copy-start.13 = (f32[64]{0:T(128)S(1)}, f32[64]{0:T(128)}, u32[]{:S(2)}) copy-start(f32[64]{0:T(128)} %get-tuple-element.511) | copy-start | bytes 772 | tf_op jit(solution)/shard_map/while
  478.5 81.2 %copy-start.9 = (f32[2,8,128]{2,1,0:T(8,128)S(1)}, f32[2,8,128]{2,1,0:T(8,128)}, u32[]{:S(2)}) copy-start(f32[2,8,128]{2,1,0:T(8,128)} %get-tuple-element.496) | copy-start | bytes 24580 | tf_op jit(solution)/shard_map/while
  478.5 81.8 %copy-start.5 = (bf16[64,64]{1,0:T(8,128)(2,1)S(1)}, bf16[64,64]{1,0:T(8,128)(2,1)}, u32[]{:S(2)}) copy-start(bf16[64,64]{1,0:T(8,128)(2,1)} %get-tuple-element.525) | copy-start | bytes 24580 | tf_op jit(solution)/shard_map/while
  559.7 0.6 copy-start.10
where the time goes:
time: 571 us; the launch traced here: 560 us
  matrix products  408 us (71%)
  local copies, waits for them, and re-layouts  56.9 us (10%)
  blocking collectives  37.4 us (7%)
  waiting for transfers between devices  22.9 us (4%)
  starting transfers between devices  17.8 us (3%)
  other arithmetic  16.8 us (3%)
    dot_general x2, matrix products, encode(): jnp.einsum('bcph,bop->bcho', weighted, feats, preferred_element_type=jnp....  172 us
    dot_general x2, matrix products, decode(): jnp.einsum('bcph,bcho->bop', weighted, folded, preferred_element_type=jnp...  161 us
    dot_general x1, matrix products, fourier(): jnp.einsum('ojlk,jlkoq->qjlk', spectrum, mode_weight, precision=highest)  32.4 us
    reshape x1, local copies, waits for them, and re-layouts, fourier(): spec_weight.reshape(spec_weight.shape[:3] + (channels, channels))  28.9 us
    dot_general x1, matrix products, fourier(): jnp.einsum('oxyz,oq->qxyz', pencil, local_weight, precision=highest)  14.5 us
    all_to_all x1, waiting for transfers between devices, local(): lax.all_to_all(send_terms.reshape(cols_count, capacity, channels, tile_ce...  13.3 us
    all_to_all x1, blocking collectives, fourier(): lax.all_to_all(returned.astype(jnp.bfloat16), 'gx', split_axis=1, concat_...  12.7 us
    all_to_all x1, blocking collectives, fourier(): lax.all_to_all(returned.astype(jnp.bfloat16), 'gy', split_axis=2, concat_...  12.5 us
  transfers between devices with their start and end apart: 4, of which 2 were waited for; matrix products, arithmetic and copies ran while one was open for 38% of the time, Pallas kernels for 0%

commit v1 on v0

v1 whole, which is shorter than its diff:
```python
import functools

import jax
import jax.numpy as jnp
import numpy as np
from jax import lax
from jax.experimental import pallas as pl
from jax.experimental.pallas import tpu as pltpu
from jax.sharding import PartitionSpec as P

G = 64
M = 32
HALF = 0.5
ROOT = 0.5**0.5
f32 = jnp.float32
bf16 = jnp.bfloat16
PLANE_ROWS = 16
MODE_ROWS = 8


def real_basis(length, modes):
    half = modes // 2
    places = np.arange(length, dtype=np.float64)[None, :]
    frequency = np.arange(half, dtype=np.float64)[:, None]
    table = np.concatenate(
        [
            np.cos(2.0 * np.pi * frequency * places / length),
            np.sin(2.0 * np.pi * (frequency + 1.0) * places / length),
        ],
        0,
    )
    return table * (2.0 / length) ** 0.5


def two_parts(matrix):
    matrix = np.asarray(matrix, np.float32)
    high = matrix.astype(bf16)
    low = (matrix - high.astype(np.float32)).astype(bf16)
    return high, low


def dot(a, b):
    return jnp.dot(a, b, preferred_element_type=f32)


def dot_rows(a, b):
    return lax.dot_general(a, b, (((1,), (1,)), ((), ())), preferred_element_type=f32)


def vmem(count):
    return [pl.BlockSpec(memory_space=pltpu.VMEM) for _ in range(count)]


def lane_left(shape, half):
    return lax.broadcasted_iota(jnp.int32, shape, len(shape) - 1) < half


def weight_table(w_ref, b_ref, cx, cy):
    xr = cx // 2
    rows = max(8, xr)
    weights = jnp.concatenate([w_ref[...], b_ref[...]], 0) * ROOT
    count = weights.shape[1]
    columns = jnp.concatenate([weights, jnp.zeros_like(weights)], 0).T
    flat = (count, 128)
    wx, wy, wz, bias = [jnp.broadcast_to(columns[:, k : k + 1], flat) for k in range(4)]
    lane = lax.broadcasted_iota(jnp.int32, flat, 1)
    slope = jnp.where(lane < 3, wx * (-cx * HALF), jnp.where(lane < 6, wy * (-cy * HALF), wz * -HALF))
    fixed = jnp.where(lane < 9, slope, wz * (0.5 * HALF) + bias)
    along_x = jnp.where(lane < 9, 0.0, wx)
    along_y = jnp.where(lane < 9, 0.0, wy)
    shape = (count, rows, 128)
    row = lax.broadcasted_iota(jnp.int32, shape, 1)
    lane = lax.broadcasted_iota(jnp.int32, shape, 2)
    at_x = ((row % xr).astype(f32) + 0.5) * HALF
    at_y = ((row // xr).astype(f32) + 0.5) * HALF
    value = fixed[:, None, :] + (at_x * along_x[:, None, :] + at_y * along_y[:, None, :])
    high = value.astype(bf16).astype(f32)
    middle = (value - high).astype(bf16).astype(f32)
    low = value - high - middle
    part = lane % 3
    table = jnp.where(part == 0, high, jnp.where(part == 1, middle, low))
    return jnp.where(lane < 12, table, 0.0).astype(bf16).reshape(count * rows, 128)


def tile_geometry(offset_rows, table, cx, cy, near_ref, base_ref):
    xr = cx // 2
    gj = max(1, 8 // xr)
    rows = gj * xr
    points = offset_rows.shape[1]
    one = jnp.ones((3, points), f32)
    parts = [offset_rows[k : k + 1] for k in range(3) for _ in range(3)] + [one]
    parts = parts + [jnp.zeros((128 - 12, points), f32)]
    base_ref[...] = dot(table, jnp.concatenate(parts, 0).astype(bf16))
    row = lax.broadcasted_iota(jnp.int32, (rows, points), 0)
    dx = ((row % xr).astype(f32) + 0.5 - cx * offset_rows[0:1]) * HALF
    dy = ((row // xr).astype(f32) + 0.5 - cy * offset_rows[1:2]) * HALF
    dz = (0.5 - offset_rows[2:3]) * HALF
    for side in range(2):
        dxs = dx + side * xr * HALF
        for group in range(cy // gj):
            dys = dy + group * gj * HALF
            start = (side * (cy // gj) + group) * rows
            near = jnp.exp(-0.5 * (dxs * dxs + dys * dys + dz * dz)) * ROOT
            near_ref[start : start + rows, :] = near


def hidden(near_ref, base_ref, w_ref, h, cx, cy):
    xr = cx // 2
    gj = max(1, 8 // xr)
    rows = gj * xr
    base = base_ref[pl.ds(pl.multiple_of(h * rows, rows), rows), :]
    step = jnp.full(base.shape, w_ref[1, h] * (gj * HALF * ROOT), f32)
    places = []
    for side in range(2):
        place = base if side == 0 else base + w_ref[0, h] * (xr * HALF * ROOT)
        for group in range(cy // gj):
            if group:
                place = place + step
            places.append(place)
    u = jnp.concatenate(places, 0)
    t = u * near_ref[...]
    return (t + t * lax.erf(u)).astype(bf16)


def offset_rows(offs_ref, block):
    return jnp.concatenate([offs_ref[a, pl.ds(block, 1), :] for a in range(3)], 0)


def encoder_body(
    cx, cy, cap, t_ref, z_ref, ws_ref, w_ref, b_ref, offs_ref, feats_ref, out_w_ref,
    pay_ref, slot_ref, places_ref, table_ref, wrow_ref, rhs_ref, near_ref, base_ref, even_ref, odd_ref,
):
    step = pl.program_id(0)
    blocks = t_ref.shape[0]
    cells = cx * cy
    rows = cells // 2
    channels, points = feats_ref.shape[1:]
    lanes = 2 * channels
    group = even_ref.shape[0]
    count = wrow_ref.shape[0] * group

    @pl.when(step == 0)
    def _():
        pay_ref[...] = jnp.zeros(pay_ref.shape, bf16)
        rhs_ref[...] = jnp.zeros(rhs_ref.shape, bf16)
        places_ref[...] = offs_ref[...].astype(f32)
        table_ref[...] = weight_table(w_ref, b_ref, cx, cy)
        out_w = out_w_ref[...].astype(f32)
        wrow_ref[...] = jnp.concatenate([out_w, out_w], 1).reshape(wrow_ref.shape)
        row = lax.broadcasted_iota(jnp.int32, (PLANE_ROWS, lanes), 0)
        for b in range(blocks):
            target = t_ref[b]
            rank = jnp.int32(0)
            for other in range(b):
                rank = rank + (t_ref[other] == target).astype(jnp.int32)
            slot_ref[b] = target * cap + rank
            here = pl.ds(cap * rows, PLANE_ROWS)
            old = pay_ref[target, here, :].astype(f32)
            pay_ref[target, here, :] = jnp.where(row == rank, z_ref[b].astype(f32), old).astype(bf16)

    for q in range(2):
        rhs_ref[q * channels : (q + 1) * channels, q * points : (q + 1) * points] = feats_ref[q]
        offset = offset_rows(places_ref, 2 * step + q)
        tile_geometry(offset, table_ref[...], cx, cy, near_ref.at[q], base_ref.at[q])

    def fill(ref, first):
        for i in range(group):
            for q in range(2):
                ref[i, q] = hidden(near_ref.at[q], base_ref.at[q], ws_ref, first + i, cx, cy)

    def drain(ref, index, total):
        left = jnp.concatenate([ref[:, q].reshape(group * cells, points) for q in range(2)], 1)
        out = dot_rows(left, rhs_ref[...])
        weights = wrow_ref[index]
        for i in range(group):
            total = total + out[i * cells : (i + 1) * cells] * weights[i : i + 1]
        return total

    def one(index, total):
        first = 2 * index * group
        fill(odd_ref, first + group)
        total = drain(even_ref, 2 * index, total)
        fill(even_ref, first + 2 * group)
        return drain(odd_ref, 2 * index + 1, total)

    pairs = count // group // 2
    fill(even_ref, 0)
    total = lax.fori_loop(0, pairs - 1, one, jnp.zeros((cells, lanes), f32))
    fill(odd_ref, count - group)
    total = drain(even_ref, 2 * pairs - 2, total)
    total = drain(odd_ref, 2 * pairs - 1, total)
    total = total * points**-0.5
    top, bottom = total[:rows], total[rows:]
    left = lane_left((rows, lanes), channels)
    made = (
        jnp.where(left, top, pltpu.roll(bottom, channels, 1)),
        jnp.where(left, pltpu.roll(top, channels, 1), bottom),
    )
    for q in range(2):
        slot = slot_ref[2 * step + q]
        target = slot // cap
        start = pl.multiple_of((slot - target * cap) * rows, rows)
        pay_ref[target, pl.ds(start, rows), :] = made[q].astype(bf16)


def encoder(targets, zstart, weight_in, bias_in, offsets, feats, out_weight, cx, cy, ny, cap):
    blocks, channels, points = feats.shape
    cells = cx * cy
    rows = cells // 2
    count = out_weight.shape[0]
    group = 8
    smem = pl.BlockSpec(memory_space=pltpu.SMEM)
    full = lambda a: pl.BlockSpec(a.shape, lambda i: (0,) * a.ndim)
    payload = (ny, cap * rows + PLANE_ROWS, 2 * channels)
    base_rows = count * max(8, cx // 2)
    return pl.pallas_call(
        functools.partial(encoder_body, cx, cy, cap),
        grid=(blocks // 2,),
        in_specs=[
            smem,
            smem,
            smem,
            full(weight_in),
            full(bias_in),
            full(offsets),
            pl.BlockSpec((2, channels, points), lambda i: (i, 0, 0)),
            full(out_weight),
        ],
        out_specs=[pl.BlockSpec(payload, lambda i: (0, 0, 0)), smem],
        out_shape=[
            jax.ShapeDtypeStruct(payload, bf16),
            jax.ShapeDtypeStruct((blocks,), jnp.int32),
        ],
        scratch_shapes=[
            pltpu.VMEM(offsets.shape, f32),
            pltpu.VMEM((base_rows, 128), bf16),
            pltpu.VMEM((count // group, group, 2 * channels), f32),
            pltpu.VMEM((2 * channels, 2 * points), bf16),
            pltpu.VMEM((2, cells, points), f32),
            pltpu.VMEM((2, base_rows, points), f32),
            pltpu.VMEM((group, 2, cells, points), bf16),
            pltpu.VMEM((group, 2, cells, points), bf16),
        ],
        name="encoder",
    )(targets, zstart, weight_in, weight_in, bias_in, offsets, feats, out_weight)


def plane_onehot(planes, cap, width):
    spread, lanes = planes.shape
    slots = spread // PLANE_ROWS * cap
    shape = (slots * width, spread)
    slot = lax.broadcasted_iota(jnp.int32, shape, 0) // width
    source = (slot // cap) * PLANE_ROWS + slot % cap
    pick = (source == lax.broadcasted_iota(jnp.int32, shape, 1)).astype(f32).astype(bf16)
    rows = dot(pick, planes)
    place = lax.broadcasted_iota(jnp.int32, rows.shape, 1).astype(f32)
    return (rows == place).astype(f32).astype(bf16)


def same_row(shape, width):
    return lax.broadcasted_iota(jnp.int32, shape, 0) % width == lax.broadcasted_iota(jnp.int32, shape, 1) % width


def slot_rows(got_ref, cap, rows, group, width):
    parts = []
    for source in range(got_ref.shape[0]):
        for q in range(cap):
            parts.append(got_ref[source, q * rows + group * width : q * rows + (group + 1) * width, :])
    return jnp.concatenate(parts, 0)


def depth_body(cap, rows, width, got_ref, high_ref, low_ref, out_ref):
    lanes = got_ref.shape[2]
    planes = got_ref[:, cap * rows :, :].reshape(-1, lanes)
    onehot = plane_onehot(planes, cap, width)
    shape = (high_ref.shape[0], onehot.shape[0])
    same = same_row(shape, width)
    high = jnp.where(same, dot_rows(high_ref[...], onehot), 0.0).astype(bf16)
    low = jnp.where(same, dot_rows(low_ref[...], onehot), 0.0).astype(bf16)
    modes = out_ref.shape[0]
    for group in range(rows // width):
        right = slot_rows(got_ref, cap, rows, group, width)
        out = dot(high, right) + dot(low, right)
        out_ref[:, group * width : (group + 1) * width, :] = out.astype(bf16).reshape(modes, width, lanes)


def depth(got, table_rows, rows, cap, width):
    lanes = got.shape[2]
    return pl.pallas_call(
        functools.partial(depth_body, cap, rows, width),
        in_specs=vmem(3),
        out_specs=vmem(1)[0],
        out_shape=jax.ShapeDtypeStruct((M, rows, lanes), bf16),
        name="depth_forward",
    )(got, *table_rows)


def skip_body(cap, rows, width, got_ref, weight_ref, bias_ref, out_ref):
    lanes = got_ref.shape[2]
    weight = weight_ref[...]
    zero = jnp.zeros_like(weight)
    pair = jnp.concatenate(
        [jnp.concatenate([weight, zero], 1), jnp.concatenate([zero, weight], 1)], 0
    )
    pair_high = pair.astype(bf16)
    pair_low = (pair - pair_high.astype(f32)).astype(bf16)
    bias = jnp.concatenate([bias_ref[...], bias_ref[...]], 1)
    planes = got_ref[:, cap * rows :, :].reshape(-1, lanes)
    onehot = plane_onehot(planes, cap, width)
    size = onehot.shape[0]
    same = same_row((size, size), width)
    shared = jnp.where(same, dot_rows(onehot, onehot), 0.0).astype(bf16)
    for group in range(rows // width):
        cells = dot(shared, slot_rows(got_ref, cap, rows, group, width))
        high = cells.astype(bf16)
        low = (cells - high.astype(f32)).astype(bf16)
        term = dot(high, pair_high) + dot(low, pair_high) + dot(high, pair_low) + bias
        out_ref[:, group * width : (group + 1) * width, :] = term.reshape(size // width, width, lanes)


def skip(got, weight, bias, rows, cap, width):
    lanes = got.shape[2]
    slots = got.shape[0] * cap
    return pl.pallas_call(
        functools.partial(skip_body, cap, rows, width),
        in_specs=vmem(3),
        out_specs=vmem(1)[0],
        out_shape=jax.ShapeDtypeStruct((slots, rows, lanes), f32),
        name="skip",
    )(got, weight, bias)


def rows_of(ref, lead, start, size):
    if size % 16 == 0:
        return ref[lead, start : start + size, :]
    return ref[lead].astype(f32)[start : start + size]


def partner(me, d, count):
    if count & (count - 1) == 0:
        return me ^ d
    return (me + d) % count


def swap_pieces(pieces, axis):
    count = len(pieces)
    moved = [pieces[0]]
    for d in range(1, count):
        pairs = [(i, partner(i, d, count)) for i in range(count)]
        moved.append(lax.ppermute(pieces[d], axis, pairs))
    return moved


def source(me, d, count):
    if count & (count - 1) == 0:
        return me ^ d
    return (me + count - d) % count


def width_body(kb, xr, nx, me_ref, in_ref, high_ref, low_ref, *rest):
    out_refs, scratch = rest[:nx], rest[nx]
    ny, total, lanes = in_ref.shape
    rows = total // kb
    inner = kb * xr
    for k in range(kb):
        right = jnp.concatenate([in_ref[y, k * rows : (k + 1) * rows, :] for y in range(ny)], 0)
        out = dot(high_ref[...], right) + dot(low_ref[...], right)
        for e in range(M):
            scratch[e * inner + k * xr : e * inner + (k + 1) * xr, :] = out[e * xr : (e + 1) * xr]
    size = M * inner // nx
    for d in range(nx):
        start = pl.multiple_of(partner(me_ref[0], d, nx) * size, size)
        out_refs[d][...] = scratch[pl.ds(start, size), :].astype(bf16)


def width_forward(me, data, table, nx, kb, xr):
    lanes = data.shape[2]
    size = M * kb * xr
    return pl.pallas_call(
        functools.partial(width_body, kb, xr, nx),
        in_specs=[pl.BlockSpec(memory_space=pltpu.SMEM)] + vmem(3),
        out_specs=vmem(nx),
        out_shape=[jax.ShapeDtypeStruct((size // nx, lanes), bf16)] * nx,
        scratch_shapes=[pltpu.VMEM((size, lanes), f32)],
        name="width_forward",
    )(me, data, *table)


def mix_body(kb, nx, me_ref, *rest):
    in_refs = rest[:nx]
    spec_ref, forward_ref, high_ref, low_ref = rest[nx : nx + 4]
    out_refs = rest[nx + 4 : 2 * nx + 4]
    pick_ref, right_ref, back_ref = rest[2 * nx + 4 :]
    lanes = in_refs[0].shape[1]
    channels = lanes // 2
    fold = MODE_ROWS // kb
    half = fold * channels

    @pl.when(pl.program_id(0) == 0)
    def _():
        shape = pick_ref.shape[1:]
        row = lax.broadcasted_iota(jnp.int32, shape, 0) % half
        lane = lax.broadcasted_iota(jnp.int32, shape, 1)
        wanted = row % channels - 2 * (row // channels) - (lane % lanes) // channels
        wanted = wanted - 2 * fold * (lane // lanes)
        for v in range(pick_ref.shape[0]):
            pick_ref[v] = (wanted == 2 * fold * v * (shape[1] // lanes)).astype(f32).astype(bf16)

    each = spec_ref.shape[1]
    inner = in_refs[0].shape[0] // each
    right = []
    for e in range(each):
        rows = slice(e * inner, (e + 1) * inner)
        for d in range(nx):
            start = pl.multiple_of(source(me_ref[0], d, nx) * inner, inner)
            right_ref[e, pl.ds(start, inner), :] = in_refs[d][rows, :].astype(f32)
        right.append(right_ref[e].astype(bf16))
    right = jnp.concatenate(right, 1)
    out = dot(forward_ref[...], jnp.concatenate([right, right], 0))
    size = M * MODE_ROWS
    left = lane_left((size, lanes), channels)
    place = (lax.broadcasted_iota(jnp.int32, (size, lanes), 0) % MODE_ROWS) // kb
    side = lax.broadcasted_iota(jnp.int32, (size, lanes), 1) // channels
    masks = [place == 2 * pair + side for pair in range(fold // 2)]
    modes = []
    for e in range(each):
        here = out[:, e * lanes : (e + 1) * lanes]
        halves = jnp.where(left, here[:size], here[size:])
        halves = halves + pltpu.roll(halves, channels, 1)
        high = halves.astype(bf16).astype(f32)
        low = halves - high
        parts = [jnp.where(mask, part, 0.0) for part in (high, low) for mask in masks]
        modes.append(jnp.concatenate(parts, 1).astype(bf16))
    modes = jnp.concatenate(modes, 0)
    totals = [jnp.zeros((M, MODE_ROWS, lanes), f32) for e in range(each)]
    width = pick_ref.shape[2] // lanes
    for v in range(pick_ref.shape[0]):
        spread = dot(modes, pick_ref[v])
        for w in range(width):
            start = (v * width + w) * MODE_ROWS
            for e in range(each):
                part = spread[e * size : (e + 1) * size, w * lanes : (w + 1) * lanes]
                part = part.reshape(M, MODE_ROWS, lanes)
                totals[e] = totals[e] + part * spec_ref[:, e, start : start + MODE_ROWS, :]
    mixed = jnp.concatenate([total.reshape(size, lanes) for total in totals], 1)
    high = mixed.astype(bf16)
    low = (mixed - high.astype(f32)).astype(bf16)
    back = dot(high_ref[...], high) + dot(high_ref[...], low) + dot(low_ref[...], high)
    count = nx * inner
    left = lane_left((count, lanes), channels)
    for e in range(each):
        here = back[:, e * lanes : (e + 1) * lanes]
        here = here + pltpu.roll(here, channels, 1)
        back_ref[e] = jnp.where(left, here[:count], here[count:])
        for d in range(nx):
            start = pl.multiple_of(partner(me_ref[0], d, nx) * inner, inner)
            out_refs[d][e * inner : (e + 1) * inner, :] = back_ref[e, pl.ds(start, inner), :].astype(bf16)


def mix(me, pieces, spec, forward, inverse, inner):
    nx = len(pieces)
    total, lanes = pieces[0].shape
    eb, kb, wide = spec.shape[1:]
    chunks = wide // lanes
    spec = spec.reshape(M, eb, kb, chunks, lanes).transpose(0, 1, 3, 2, 4).reshape(M, eb, chunks * kb, lanes)
    full = lambda a: pl.BlockSpec(a.shape, lambda e: (0,) * a.ndim)
    each = 2 if eb % 2 == 0 else 1
    piece = pl.BlockSpec((each * inner, lanes), lambda e: (e, 0))
    fold = MODE_ROWS // kb
    return pl.pallas_call(
        functools.partial(mix_body, kb, nx),
        grid=(eb // each,),
        in_specs=[pl.BlockSpec(memory_space=pltpu.SMEM)]
        + [piece] * nx
        + [
            pl.BlockSpec((M, each) + spec.shape[2:], lambda e: (0, e, 0, 0)),
            full(forward),
            full(inverse[0]),
            full(inverse[1]),
        ],
        out_specs=[piece] * nx,
        out_shape=[jax.ShapeDtypeStruct((total, lanes), bf16)] * nx,
        scratch_shapes=[
            pltpu.VMEM((chunks // fold // 2, fold * lanes, 2 * lanes), bf16),
            pltpu.VMEM((each, nx * inner, lanes), f32),
            pltpu.VMEM((each, nx * inner, lanes), f32),
        ],
        name="mix",
    )(me, *pieces, spec, forward, *inverse)


def width_back_body(kb, xr, nx, me_ref, *rest):
    in_refs = rest[:nx]
    high_ref, low_ref, out_ref, right_ref, made_ref = rest[nx:]
    total, lanes = in_refs[0].shape
    ny = out_ref.shape[0]
    inner = kb * xr
    for d in range(nx):
        start = pl.multiple_of(source(me_ref[0], d, nx) * total, total)
        right_ref[pl.ds(start, total), :] = in_refs[d][...].astype(f32)
    for k in range(kb):
        right = jnp.concatenate(
            [right_ref[e * inner + k * xr : e * inner + (k + 1) * xr, :] for e in range(M)], 0
        ).astype(bf16)
        out = dot(high_ref[...], right) + dot(low_ref[...], right)
        for y in range(G):
            made_ref[y * inner + k * xr : y * inner + (k + 1) * xr, :] = out[y * xr : (y + 1) * xr]
    out_ref[...] = made_ref[...].astype(bf16).reshape(out_ref.shape)


def width_back(me, pieces, table, ny, kb, xr):
    nx = len(pieces)
    lanes = pieces[0].shape[1]
    inner = kb * xr
    return pl.pallas_call(
        functools.partial(width_back_body, kb, xr, nx),
        in_specs=[pl.BlockSpec(memory_space=pltpu.SMEM)] + vmem(nx + 2),
        out_specs=vmem(1)[0],
        out_shape=jax.ShapeDtypeStruct((ny, G // ny * inner, lanes), bf16),
        scratch_shapes=[pltpu.VMEM((M * inner, lanes), f32), pltpu.VMEM((G * inner, lanes), f32)],
        name="width_back",
    )(me, *pieces, *table)


def latent_body(cap, inner, xr, in_ref, planes_ref, skip_ref, high_ref, low_ref, out_ref, scratch):
    ny, total, lanes = in_ref.shape
    slots = skip_ref.shape[0]
    onehot = plane_onehot(planes_ref[...].reshape(-1, lanes), cap, xr)
    shape = (onehot.shape[0], high_ref.shape[0])
    same = same_row(shape, xr)
    high = jnp.where(same, dot_rows(onehot, high_ref[...]), 0.0).astype(bf16)
    low = jnp.where(same, dot_rows(onehot, low_ref[...]), 0.0).astype(bf16)
    for j in range(total // inner):
        right = jnp.concatenate([rows_of(in_ref, t, j * inner, inner) for t in range(ny)], 0).astype(bf16)
        out = (dot(high, right) + dot(low, right)).reshape(slots, xr, lanes)
        here = slice(j * xr, (j + 1) * xr)
        out = out + skip_ref[:, here, :]
        scratch[:, here, :] = 0.5 * out * (1.0 + lax.erf(out * ROOT))
    out_ref[...] = scratch[...].astype(bf16)


def latent_tiles(data, got, skipped, table_rows, cap, rows, inner, xr):
    ny, _, lanes = data.shape
    full = lambda a: pl.BlockSpec(a.shape, lambda i: (0,) * a.ndim)
    return pl.pallas_call(
        functools.partial(latent_body, cap, inner, xr),
        grid=(1,),
        in_specs=[
            full(data),
            pl.BlockSpec((ny, PLANE_ROWS, lanes), lambda i: (0, cap * rows // PLANE_ROWS, 0)),
            full(skipped),
            full(table_rows[0]),
            full(table_rows[1]),
        ],
        out_specs=pl.BlockSpec(skipped.shape, lambda i: (0, 0, 0)),
        out_shape=jax.ShapeDtypeStruct(skipped.shape, bf16),
        scratch_shapes=[pltpu.VMEM(skipped.shape, f32)],
        name="latent",
    )(data, got, skipped, *table_rows)


STEP = 2


def spread_body(out_w_ref, head_ref, wcol_ref, wide_ref):
    count, channels, cells = wcol_ref.shape
    columns = out_w_ref[...].astype(f32).T
    for h in range(count):
        wcol_ref[h] = jnp.broadcast_to(columns[:, h : h + 1], (channels, cells)).astype(bf16)
    wide_ref[...] = jnp.broadcast_to(head_ref[...], (wide_ref.shape[1], channels)).T


def spread(out_weight, head, cells, points):
    count, channels = out_weight.shape
    return pl.pallas_call(
        spread_body,
        in_specs=vmem(2),
        out_specs=vmem(2),
        out_shape=[
            jax.ShapeDtypeStruct((count, channels, cells), bf16),
            jax.ShapeDtypeStruct((channels, points), f32),
        ],
        name="spread",
    )(out_weight, head)


def ahead_body(cx, cy, group, first, ws_ref, w_ref, b_ref, offs_ref, *rest):
    hidden_ref, places_ref, table_ref, near_ref, base_ref = rest[-5:]
    cells = cx * cy
    step = pl.program_id(0)

    @pl.when(step == 0)
    def _():
        places_ref[...] = offs_ref[...].astype(f32)
        table_ref[...] = weight_table(w_ref, b_ref, cx, cy)

    tile_geometry(offset_rows(places_ref, step + first), table_ref[...], cx, cy, near_ref, base_ref)

    def one(index, carry):
        for i in range(group):
            h = index * group + i
            start = pl.multiple_of(h * cells, cells)
            hidden_ref[0, pl.ds(start, cells), :] = hidden(near_ref, base_ref, ws_ref, h, cx, cy)
        return carry

    lax.fori_loop(0, b_ref.shape[1] // group, one, 0)


def ahead(weight_in, bias_in, offsets, cx, cy, first, number, old):
    _, blocks, points = offsets.shape
    cells = cx * cy
    count = bias_in.shape[1]
    full = lambda a: pl.BlockSpec(a.shape, lambda i: (0,) * a.ndim)
    made = (blocks, count * cells, points)
    base_rows = count * max(8, cx // 2)
    return pl.pallas_call(
        functools.partial(ahead_body, cx, cy, 16, first),
        grid=(number,),
        in_specs=[pl.BlockSpec(memory_space=pltpu.SMEM), full(weight_in), full(bias_in), full(offsets)]
        + [pl.BlockSpec(memory_space=pl.ANY)] * len(old),
        out_specs=pl.BlockSpec((1,) + made[1:], lambda i: (i + first, 0, 0)),
        out_shape=jax.ShapeDtypeStruct(made, bf16),
        scratch_shapes=[
            pltpu.VMEM(offsets.shape, f32),
            pltpu.VMEM((base_rows, 128), bf16),
            pltpu.VMEM((cells, points), f32),
            pltpu.VMEM((base_rows, points), f32),
        ],
        input_output_aliases={4: 0} if old else {},
        name="ahead",
    )(weight_in, weight_in, bias_in, offsets, *old)


def decoder_body(cells, group, slot_ref, *rest):
    tile_refs = rest[:STEP]
    ready_ref, wcol_ref, wide_ref, out_ref = rest[STEP:]
    step = pl.program_id(0)
    count, channels, _ = wcol_ref.shape
    points = ready_ref.shape[2]

    def tile_of(ref):
        tile = ref[0].astype(f32).T
        return jnp.concatenate([tile[:channels], tile[channels:]], 1).astype(bf16)

    tiles = [tile_of(ref) for ref in tile_refs]

    def one(index, totals):
        first = index * group
        start = pl.multiple_of(first * cells, group * cells)
        out = []
        for q in range(STEP):
            folded = jnp.concatenate([tiles[q] * wcol_ref[first + i] for i in range(group)], 1)
            out.append(totals[q] + dot(folded, ready_ref[q, pl.ds(start, group * cells), :]))
        return tuple(out)

    zero = jnp.zeros((channels, points), f32)
    totals = lax.fori_loop(0, count // group, one, (zero,) * STEP)
    for q in range(STEP):
        values = totals[q] * cells**-0.5
        active = 0.5 * values * (1.0 + lax.erf(values * ROOT))
        row = jnp.sum(active * wide_ref[...], axis=0, keepdims=True)
        out_ref[pl.ds(STEP * step + q, 1), :] = row


def decoder(slots, tiles, ready, wcol, wide, cells):
    blocks, _, points = ready.shape
    group = 16
    full = lambda a: pl.BlockSpec(a.shape, lambda b, s: (0,) * a.ndim)
    tile = (1,) + tiles.shape[1:]

    def tile_spec(q):
        return pl.BlockSpec(tile, lambda b, s: (s[STEP * b + q], 0, 0))

    return pl.pallas_call(
        functools.partial(decoder_body, cells, group),
        grid_spec=pltpu.PrefetchScalarGridSpec(
            num_scalar_prefetch=1,
            grid=(blocks // STEP,),
            in_specs=[tile_spec(q) for q in range(STEP)]
            + [
                pl.BlockSpec((STEP,) + ready.shape[1:], lambda b, s: (b, 0, 0)),
                full(wcol),
                full(wide),
            ],
            out_specs=pl.BlockSpec((blocks, points), lambda b, s: (0, 0)),
        ),
        out_shape=jax.ShapeDtypeStruct((blocks, points), f32),
        name="decoder",
    )(slots, *([tiles] * STEP), ready, wcol, wide)


def local(
    point_feats,
    offsets,
    targets,
    zstart,
    enc_in,
    enc_bias,
    enc_out,
    dec_in,
    dec_bias,
    dec_out,
    spec_weight,
    local_weight,
    local_bias,
    head_weight,
):
    nx = lax.axis_size("gx")
    ny = lax.axis_size("gy")
    cx = G // nx
    cy = G // ny
    rows = cx * cy // 2
    xr = cx // 2
    kb = M // ny
    inner = kb * xr
    blocks, channels, points = point_feats.shape
    lanes = 2 * channels
    cap = max(2, 2 * blocks // ny)
    fold = MODE_ROWS // kb

    table = real_basis(G, M)
    eye = np.eye
    depth_table = np.zeros((M, lanes))
    depth_table[:, :G] = table
    depth_rows = two_parts(np.repeat(depth_table, 16, 0))
    depth_back_rows = two_parts(np.repeat(depth_table, xr, 0))
    width_table = two_parts(np.kron(table, eye(xr)))
    width_back_table = two_parts(np.kron(table.T, eye(xr)))
    by_x = table.reshape(M, nx, 2, xr)
    copies = np.tile(eye(kb), (fold, 1))
    length_table = np.einsum("aBvr,fk->vafBkr", by_x, copies).reshape(2 * M * MODE_ROWS, nx * inner)
    length_forward = np.concatenate(two_parts(length_table), 1)
    length_back = two_parts(
        np.einsum("aBvr,fk->vBkraf", by_x, copies).reshape(2 * nx * inner, M * MODE_ROWS)
    )

    swap = functools.partial(lax.all_to_all, split_axis=0, concat_axis=0, tiled=True)
    me = lax.axis_index("gx").astype(jnp.int32).reshape(1)
    offs = jnp.transpose(offsets, (1, 0, 2))

    payload, slots = encoder(
        targets[:, 0], zstart, enc_in, enc_bias[None, :], offs, point_feats, enc_out, cx, cy, ny, cap
    )
    third = blocks // 3
    made = functools.partial(ahead, dec_in, dec_bias[None, :], offs, cx, cy)
    got = swap(payload, "gy")
    ready = made(0, third, ())
    got, ready = lax.optimization_barrier((got, ready))
    data = depth(got, depth_rows, rows, cap, 16)
    ready = made(third, third, (ready,))
    data = swap(data.reshape(ny, kb * rows, lanes), "gy")
    data, ready = lax.optimization_barrier((data, ready))
    wcol, wide = spread(dec_out, head_weight[None, :], cx * cy, points)
    skipped = skip(got, local_weight, local_bias[None, :], rows, cap, 16)
    pieces = width_forward(me, data, width_table, nx, kb, xr)
    pieces = swap_pieces(pieces, "gx")
    pieces = mix(me, pieces, spec_weight, length_forward, length_back, inner)
    pieces = swap_pieces(pieces, "gx")
    data = width_back(me, pieces, width_back_table, ny, kb, xr)
    data = swap(data, "gy")
    data, skipped, wcol, wide = lax.optimization_barrier((data, skipped, wcol, wide))
    tiles = latent_tiles(data, got, skipped, depth_back_rows, cap, rows, inner, xr)
    ready = made(2 * third, blocks - 2 * third, (ready,))
    tiles = swap(tiles.reshape(ny, cap * rows, lanes), "gy")
    tiles = tiles.reshape(ny * cap, rows, lanes)
    return decoder(slots, tiles, ready, wcol, wide, cx * cy)


def solution(mesh):
    placed = (
        P(("gx", "gy"), None, None),
        P(("gx", "gy"), None, None),
        P(("gx", "gy"), None),
        P(("gx", "gy")),
        P(),
        P(),
        P(),
        P(),
        P(),
        P(),
        P(None, "gx", "gy", None),
        P(),
        P(),
        P(),
    )
    return jax.shard_map(
        local, mesh=mesh, in_specs=placed, out_specs=P(("gx", "gy"), None), check_vma=False
    )
```

time: 571 us -> 145 us (0.25); the launches traced: 560 us -> 144 us
  matrix products: 408 us -> 0 us
  Pallas kernels: 0 us -> 99.6 us
  local copies, waits for them, and re-layouts: 56.9 us -> 4.48 us
  blocking collectives: 37.4 us -> 0 us
  other arithmetic: 16.8 us -> 0 us
  waiting for transfers between devices: 22.9 us -> 15.4 us
  starting transfers between devices: 17.8 us -> 24.9 us
    dot_general x19 -> x0, matrix products: 408 us -> none  [the longest x2 172 us: encode(): jnp.einsum('bcph,bop->bcho', weighted, feats, preferred_element_type=jnp....]
    pallas_call x0 -> x12, Pallas kernels: none -> 99.6 us  [the longest x3 26.4 us: ahead(): pl.pallas_call(functools.partial(ahead_body, cx, cy, 16, first), grid=(nu...]
    all_to_all x3 -> x0, blocking collectives: 37.4 us -> none  [the longest x1 12.7 us: fourier(): lax.all_to_all(returned.astype(jnp.bfloat16), 'gx', split_axis=1, concat_...]
    reshape x2 -> x0, local copies, waits for them, and re-layouts: 29.9 us -> none  [the longest x1 28.9 us: fourier(): spec_weight.reshape(spec_weight.shape[:3] + (channels, channels))]
    all_to_all x4, waiting for transfers between devices: 22.9 us -> 5.81 us  [the longest x1 2.84 us: local(): data = swap(data, 'gy')]
    ppermute x0 -> x6, waiting for transfers between devices: none -> 9.56 us  [swap_pieces(): moved.append(lax.ppermute(pieces[d], axis, pairs))]
    ppermute x0 -> x6, starting transfers between devices: none -> 8.83 us  [swap_pieces(): moved.append(lax.ppermute(pieces[d], axis, pairs))]
  transfers between devices with their start and end apart: 4 -> 10, of which waited for: 2 -> 10; matrix products, arithmetic and copies ran while one was open for 38% -> 0% of each run, Pallas kernels for 0% -> 23%
where the time goes in v1:
time: 145 us; the launch traced here: 144 us
  Pallas kernels  99.6 us (69%)
  starting transfers between devices  24.9 us (17%)
  waiting for transfers between devices  15.4 us (11%)
  local copies, waits for them, and re-layouts  4.48 us (3%)
    pallas_call x3, Pallas kernels, ahead(): pl.pallas_call(functools.partial(ahead_body, cx, cy, 16, first), grid=(nu...  26.4 us
    pallas_call x1, Pallas kernels, encoder(): pl.pallas_call(functools.partial(encoder_body, cx, cy, cap), grid=(blocks...  25.8 us
    pallas_call x1, Pallas kernels, decoder(): pl.pallas_call(functools.partial(decoder_body, cells, group), grid_spec=p...  18.3 us
    pallas_call x1, Pallas kernels, mix(): pl.pallas_call(functools.partial(mix_body, kb, nx), grid=(eb // each,), i...  10 us
    ppermute x6, waiting for transfers between devices, swap_pieces(): moved.append(lax.ppermute(pieces[d], axis, pairs))  9.56 us
    ppermute x6, starting transfers between devices, swap_pieces(): moved.append(lax.ppermute(pieces[d], axis, pairs))  8.83 us
    all_to_all x1, starting transfers between devices, local(): got = swap(payload, 'gy')  5.22 us
    pallas_call x1, Pallas kernels, skip(): pl.pallas_call(functools.partial(skip_body, cap, rows, width), in_specs=v...  4.62 us
  transfers between devices with their start and end apart: 10, of which 10 were waited for; matrix products, arithmetic and copies ran while one was open for 0% of the time, Pallas kernels for 23%

profile of v1, /device:TPU:0, one launch (start us, length us, event | category | flops | bytes accessed | tf_op | source)
XLA Modules:
  0.0 144.4 jit_solution(308101964907715486)
XLA Ops:
  0.0 25.8 %encoder.1 = (bf16[8,272,128]{2,1,0:T(8,128)(2,1)}, s32[16]{0:T(128)}) custom-call(s32[16]{0:T(128)} %bitcast.27, s32[16]{0:T(128)} %z_ref.1, f32[3,64]{1,0:T(4,128)} %w_ref.4, f32[3,64]{1,0:T(4,128)} %w_ref.4, f32[1,64]{1,0:T(1,128)} %bitcast.28, bf16[3,16,128]{2,1,0:T(8,128)(2,1)} %bitcast.20, bf16[16,64,128]{2,1,0:T(8,128)(2,1)} %feats_ref.1, ...), custom_call_target="tpu_custom_call" | custom-call | tf_op jit(solution)/shard_map/encoder/pallas_call | solution.py:216
  25.8 5.2 %all-to-all-start = ((bf16[8,272,128]{2,1,0:T(8,128)(2,1)}), bf16[8,272,128]{2,1,0:T(8,128)(2,1)S(1)}, u32[]{:S(2)}, u32[]{:S(2)}) async-start(bf16[8,272,128]{2,1,0:T(8,128)(2,1)} %get-tuple-element.26), calls=%async_computation | async-start | bytes 1114112 | tf_op jit(solution)/shard_map/all_to_all | solution.py:746
  31.0 8.5 %ahead.3.rest_0_ = bf16[16,8192,128]{2,1,0:T(8,128)(2,1)} custom-call(f32[3,64]{1,0:T(4,128)} %w_ref.7, f32[3,64]{1,0:T(4,128)} %w_ref.7, f32[1,64]{1,0:T(1,128)} %bitcast.24, bf16[3,16,128]{2,1,0:T(8,128)(2,1)} %bitcast.21), custom_call_target="tpu_custom_call" | custom-call | tf_op jit(solution)/shard_map/ahead/pallas_call | solution.py:616
  39.5 1.6 %all-to-all-done.got_ref.planes_ref = bf16[8,272,128]{2,1,0:T(8,128)(2,1)S(1)} async-done(((bf16[8,272,128]{2,1,0:T(8,128)(2,1)}), bf16[8,272,128]{2,1,0:T(8,128)(2,1)S(1)}, u32[]{:S(2)}, u32[]{:S(2)}) %all-to-all-start) | async-done | bytes 557088 | tf_op jit(solution)/shard_map/all_to_all | solution.py:746
  41.1 0.0 copy-start
  41.1 0.8 copy-done
  41.9 3.6 %depth_forward.1 = bf16[32,64,128]{2,1,0:T(8,128)(2,1)} custom-call(bf16[8,272,128]{2,1,0:T(8,128)(2,1)} %copy-done, bf16[512,128]{1,0:T(8,128)(2,1)} %constant.27.clone.high_ref, bf16[512,128]{1,0:T(8,128)(2,1)} %constant.28.clone.low_ref), custom_call_target="tpu_custom_call" | custom-call | tf_op jit(solution)/shard_map/depth_forward/pallas_call | solution.py:289
  45.5 3.5 %all-to-all-start.1 = ((bf16[8,256,128]{2,1,0:T(8,128)(2,1)}), bf16[8,256,128]{2,1,0:T(8,128)(2,1)S(1)}, u32[]{:S(2)}, u32[]{:S(2)}) async-start(bf16[8,256,128]{2,1,0:T(8,128)(2,1)} %bitcast.18), calls=%async_computation.1 | async-start | bytes 1048576 | tf_op jit(solution)/shard_map/all_to_all | solution.py:751
  49.0 8.3 %ahead.4.rest_0_ = bf16[16,8192,128]{2,1,0:T(8,128)(2,1)} custom-call(f32[3,64]{1,0:T(4,128)} %w_ref.7, f32[3,64]{1,0:T(4,128)} %w_ref.7, f32[1,64]{1,0:T(1,128)} %bitcast.25, bf16[3,16,128]{2,1,0:T(8,128)(2,1)} %bitcast.22, bf16[16,8192,128]{2,1,0:T(8,128)(2,1)} %ahead.3.rest_0_), custom_call_target="tpu_custom_call", output_to_operand_aliasing={{}: (4, {})} | custom-call | tf_op jit(solution)/shard_map/ahead/pallas_call | solution.py:616
  57.4 1.3 all-to-all-done.1.in_ref
  58.7 0.8 copy-done.2
  59.5 2.6 %width_forward.1 = (bf16[256,128]{1,0:T(8,128)(2,1)}, bf16[256,128]{1,0:T(8,128)(2,1)}, bf16[256,128]{1,0:T(8,128)(2,1)}, bf16[256,128]{1,0:T(8,128)(2,1)}) custom-call(s32[1]{0:T(128)} %bitcast.3.me_ref, bf16[8,256,128]{2,1,0:T(8,128)(2,1)} %copy-done.2, bf16[256,512]{1,0:T(8,128)(2,1)} %constant.29.clone.high_ref, bf16[256,512]{1,0:T(8,128)(2,1)} %constant.30.clone.low_ref), custom_call_target="tpu_custom_call" | custom-call | tf_op jit(solution)/shard_map/width_forward/pallas_call | solution.py:379
  62.1 1.6 %collective-permute-start = (bf16[256,128]{1,0:T(8,128)(2,1)}, bf16[256,128]{1,0:T(8,128)(2,1)S(1)}, u32[]{:S(2)}, u32[]{:S(2)}) collective-permute-start(bf16[256,128]{1,0:T(8,128)(2,1)} %get-tuple-element.31), channel_id=1, source_target_pairs={{0,8},{8,0},{16,24},{24,16},{1,9},{9,1},{17,25},{25,17},{2,10},{10... | collective-permute-start | bytes 196616 | tf_op jit(solution)/shard_map/ppermute | solution.py:350
  63.6 2.6 %collective-permute-start.1 = (bf16[256,128]{1,0:T(8,128)(2,1)}, bf16[256,128]{1,0:T(8,128)(2,1)S(1)}, u32[]{:S(2)}, u32[]{:S(2)}) collective-permute-start(bf16[256,128]{1,0:T(8,128)(2,1)} %get-tuple-element.32), channel_id=1, source_target_pairs={{0,16},{8,24},{16,0},{24,8},{1,17},{9,25},{17,1},{25,9},{2,18},{10... | collective-permute-start | bytes 196616 | tf_op jit(solution)/shard_map/ppermute | solution.py:350
  66.2 0.2 collective-permute-start.2
  66.4 0.7 collective-permute-done.rest_1_
  67.2 0.0 copy-start.4
  67.2 3.2 %collective-permute-done.1.rest_2_ = bf16[256,128]{1,0:T(8,128)(2,1)S(1)} collective-permute-done((bf16[256,128]{1,0:T(8,128)(2,1)}, bf16[256,128]{1,0:T(8,128)(2,1)S(1)}, u32[]{:S(2)}, u32[]{:S(2)}) %collective-permute-start.1) | collective-permute-done | bytes 65568 | tf_op jit(solution)/shard_map/ppermute | solution.py:350
  70.4 0.0 copy-start.5
  70.4 2.1 %collective-permute-done.2.rest_3_ = bf16[256,128]{1,0:T(8,128)(2,1)S(1)} collective-permute-done((bf16[256,128]{1,0:T(8,128)(2,1)}, bf16[256,128]{1,0:T(8,128)(2,1)S(1)}, u32[]{:S(2)}, u32[]{:S(2)}) %collective-permute-start.2) | collective-permute-done | bytes 65568 | tf_op jit(solution)/shard_map/ppermute | solution.py:350
  72.5 0.0 copy-start.6
  72.5 0.0 copy-done.4
  72.5 0.0 copy-done.5
  72.5 0.6 copy-done.6
  73.1 10.0 %mix.1 = (bf16[256,128]{1,0:T(8,128)(2,1)}, bf16[256,128]{1,0:T(8,128)(2,1)}, bf16[256,128]{1,0:T(8,128)(2,1)}, bf16[256,128]{1,0:T(8,128)(2,1)}) custom-call(s32[1]{0:T(128)} %bitcast.3.me_ref, bf16[256,128]{1,0:T(8,128)(2,1)} %get-tuple-element.30.rest_0_, bf16[256,128]{1,0:T(8,128)(2,1)} %copy-done.4, bf16[256,128]{1,0:T(8,128)(2,1)} %copy-done.5, ...), custom_call_target="tpu_custom_call" | custom-call | tf_op jit(solution)/shard_map/mix/pallas_call | solution.py:470
  83.2 0.1 collective-permute-start.3
  83.2 1.6 %collective-permute-start.4 = (bf16[256,128]{1,0:T(8,128)(2,1)}, bf16[256,128]{1,0:T(8,128)(2,1)S(1)}, u32[]{:S(2)}, u32[]{:S(2)}) collective-permute-start(bf16[256,128]{1,0:T(8,128)(2,1)} %get-tuple-element.36), channel_id=1, source_target_pairs={{0,16},{8,24},{16,0},{24,8},{1,17},{9,25},{17,1},{25,9},{2,18},{10... | collective-permute-start | bytes 196616 | tf_op jit(solution)/shard_map/ppermute | solution.py:350
  84.9 2.8 %collective-permute-start.5 = (bf16[256,128]{1,0:T(8,128)(2,1)}, bf16[256,128]{1,0:T(8,128)(2,1)S(1)}, u32[]{:S(2)}, u32[]{:S(2)}) collective-permute-start(bf16[256,128]{1,0:T(8,128)(2,1)} %get-tuple-element.37), channel_id=1, source_target_pairs={{0,24},{8,16},{16,8},{24,0},{1,25},{9,17},{17,9},{25,1},{2,26},{10... | collective-permute-start | bytes 196616 | tf_op jit(solution)/shard_map/ppermute | solution.py:350
  87.6 0.4 collective-permute-done.3.rest_1_
  88.0 0.0 copy-start.7
  88.0 0.7 collective-permute-done.4.rest_2_
  88.7 0.0 copy-start.8
  88.7 2.4 %collective-permute-done.5.rest_3_ = bf16[256,128]{1,0:T(8,128)(2,1)S(1)} collective-permute-done((bf16[256,128]{1,0:T(8,128)(2,1)}, bf16[256,128]{1,0:T(8,128)(2,1)S(1)}, u32[]{:S(2)}, u32[]{:S(2)}) %collective-permute-start.5) | collective-permute-done | bytes 65568 | tf_op jit(solution)/shard_map/ppermute | solution.py:350
  91.1 0.0 copy-done.7
  91.1 0.0 copy-done.8
  91.1 0.6 copy-done.9
  91.7 2.7 %width_back.1 = bf16[8,256,128]{2,1,0:T(8,128)(2,1)} custom-call(s32[1]{0:T(128)} %bitcast.3.me_ref, bf16[256,128]{1,0:T(8,128)(2,1)} %get-tuple-element.34.rest_0_, bf16[256,128]{1,0:T(8,128)(2,1)} %copy-done.7, bf16[256,128]{1,0:T(8,128)(2,1)} %copy-done.8, bf16[256,128]{1,0:T(8,128)(2,1)} %copy-done.9, bf16[512,256]{1,0:T(8,128)(2,1)} %constant.34.clone.rest_4_, ...), custom_call_target="tpu_custom_call" | custom-call | tf_op jit(solution)/shard_map/width_back/pallas_call | solution.py:515
  94.5 3.8 %all-to-all-start.2 = ((bf16[8,256,128]{2,1,0:T(8,128)(2,1)}), bf16[8,256,128]{2,1,0:T(8,128)(2,1)S(1)}, u32[]{:S(2)}, u32[]{:S(2)}) async-start(bf16[8,256,128]{2,1,0:T(8,128)(2,1)} %width_back.1), calls=%async_computation.2 | async-start | bytes 1048576 | tf_op jit(solution)/shard_map/all_to_all | solution.py:760
  98.3 2.3 %spread.1 = (bf16[64,64,128]{2,1,0:T(8,128)(2,1)}, f32[64,128]{1,0:T(8,128)}) custom-call(bf16[64,64]{1,0:T(8,128)(2,1)} %out_w_ref.3, f32[1,64]{1,0:T(1,128)} %bitcast.30), custom_call_target="tpu_custom_call" | custom-call | tf_op jit(solution)/shard_map/spread/pallas_call | solution.py:575
  100.6 4.6 %skip.1.skip_ref = f32[32,64,128]{2,1,0:T(8,128)} custom-call(bf16[8,272,128]{2,1,0:T(8,128)(2,1)} %copy-done, f32[64,64]{1,0:T(8,128)} %weight_ref.1, f32[1,64]{1,0:T(1,128)} %bitcast.29), custom_call_target="tpu_custom_call" | custom-call | tf_op jit(solution)/shard_map/skip/pallas_call | solution.py:324
  105.2 2.8 %all-to-all-done.2.in_ref = bf16[8,256,128]{2,1,0:T(8,128)(2,1)S(1)} async-done(((bf16[8,256,128]{2,1,0:T(8,128)(2,1)}), bf16[8,256,128]{2,1,0:T(8,128)(2,1)S(1)}, u32[]{:S(2)}, u32[]{:S(2)}) %all-to-all-start.2) | async-done | bytes 524320 | tf_op jit(solution)/shard_map/all_to_all | solution.py:760
  108.0 0.8 copy-done.3
  108.8 3.2 %latent.1 = bf16[32,64,128]{2,1,0:T(8,128)(2,1)} custom-call(bf16[8,256,128]{2,1,0:T(8,128)(2,1)} %copy-done.3, bf16[8,272,128]{2,1,0:T(8,128)(2,1)} %copy-done, f32[32,64,128]{2,1,0:T(8,128)} %skip.1.skip_ref, bf16[256,128]{1,0:T(8,128)(2,1)} %constant.36.clone.high_ref, bf16[256,128]{1,0:T(8,128)(2,1)} %constant.37.clone.low_ref), custom_call_target="tpu_custom_call" | custom-call | tf_op jit(solution)/shard_map/latent/pallas_call | solution.py:545
  112.0 3.5 %all-to-all-start.3 = ((bf16[8,256,128]{2,1,0:T(8,128)(2,1)}), bf16[8,256,128]{2,1,0:T(8,128)(2,1)S(1)}, u32[]{:S(2)}, u32[]{:S(2)}) async-start(bf16[8,256,128]{2,1,0:T(8,128)(2,1)} %bitcast.19), calls=%async_computation.3 | async-start | bytes 1048576 | tf_op jit(solution)/shard_map/all_to_all | solution.py:764
  115.5 9.6 %ahead.5.rest_2_ = bf16[16,8192,128]{2,1,0:T(8,128)(2,1)} custom-call(f32[3,64]{1,0:T(4,128)} %w_ref.7, f32[3,64]{1,0:T(4,128)} %w_ref.7, f32[1,64]{1,0:T(1,128)} %bitcast.26, bf16[3,16,128]{2,1,0:T(8,128)(2,1)} %bitcast.23, bf16[16,8192,128]{2,1,0:T(8,128)(2,1)} %ahead.4.rest_0_), custom_call_target="tpu_custom_call", output_to_operand_aliasing={{}: (4, {})} | custom-call | tf_op jit(solution)/shard_map/ahead/pallas_call | solution.py:616
  125.1 0.1 all-to-all-done.3
  125.2 0.8 copy-done.1
  126.0 18.3 %decoder.1 = f32[16,128]{1,0:T(8,128)} custom-call(s32[16]{0:T(128)} %get-tuple-element.25.slot_ref, bf16[32,64,128]{2,1,0:T(8,128)(2,1)} %bitcast.16, bf16[32,64,128]{2,1,0:T(8,128)(2,1)} %bitcast.17, bf16[16,8192,128]{2,1,0:T(8,128)(2,1)} %ahead.5.rest_2_, bf16[64,64,128]{2,1,0:T(8,128)(2,1)} %get-tuple-element.43.rest_3_, f32[64,128]{1,0:T(8,128)} %get-tuple-element.44.rest_4_), custom_call_target="tpu_custom_call" | custom-call | tf_op jit(solution)/shard_map/decoder/pallas_call | solution.py:674
  (4 shorter events, 0.0 us)
Async XLA Ops:
  25.8 15.3 %all-to-all-start = ((bf16[8,272,128]{2,1,0:T(8,128)(2,1)}), bf16[8,272,128]{2,1,0:T(8,128)(2,1)S(1)}, u32[]{:S(2)}, u32[]{:S(2)}) async-start(bf16[8,272,128]{2,1,0:T(8,128)(2,1)} %get-tuple-element.26), calls=%async_computation | async-start | bytes 1114112 | tf_op jit(solution)/shard_map/all_to_all | solution.py:746
  41.1 0.8 copy-start
  45.5 13.1 %all-to-all-start.1 = ((bf16[8,256,128]{2,1,0:T(8,128)(2,1)}), bf16[8,256,128]{2,1,0:T(8,128)(2,1)S(1)}, u32[]{:S(2)}, u32[]{:S(2)}) async-start(bf16[8,256,128]{2,1,0:T(8,128)(2,1)} %bitcast.18), calls=%async_computation.1 | async-start | bytes 1048576 | tf_op jit(solution)/shard_map/all_to_all | solution.py:751
  58.7 0.8 copy-start.2
  62.1 5.1 %collective-permute-start = (bf16[256,128]{1,0:T(8,128)(2,1)}, bf16[256,128]{1,0:T(8,128)(2,1)S(1)}, u32[]{:S(2)}, u32[]{:S(2)}) collective-permute-start(bf16[256,128]{1,0:T(8,128)(2,1)} %get-tuple-element.31), channel_id=1, source_target_pairs={{0,8},{8,0},{16,24},{24,16},{1,9},{9,1},{17,25},{25,17},{2,10},{10... | collective-permute-start | bytes 196616 | tf_op jit(solution)/shard_map/ppermute | solution.py:350
  63.6 6.8 %collective-permute-start.1 = (bf16[256,128]{1,0:T(8,128)(2,1)}, bf16[256,128]{1,0:T(8,128)(2,1)S(1)}, u32[]{:S(2)}, u32[]{:S(2)}) collective-permute-start(bf16[256,128]{1,0:T(8,128)(2,1)} %get-tuple-element.32), channel_id=1, source_target_pairs={{0,16},{8,24},{16,0},{24,8},{1,17},{9,25},{17,1},{25,9},{2,18},{10... | collective-permute-start | bytes 196616 | tf_op jit(solution)/shard_map/ppermute | solution.py:350
  66.2 6.3 %collective-permute-start.2 = (bf16[256,128]{1,0:T(8,128)(2,1)}, bf16[256,128]{1,0:T(8,128)(2,1)S(1)}, u32[]{:S(2)}, u32[]{:S(2)}) collective-permute-start(bf16[256,128]{1,0:T(8,128)(2,1)} %get-tuple-element.33), channel_id=1, source_target_pairs={{0,24},{8,16},{16,8},{24,0},{1,25},{9,17},{17,9},{25,1},{2,26},{10... | collective-permute-start | bytes 196616 | tf_op jit(solution)/shard_map/ppermute | solution.py:350
  67.2 5.3 %copy-start.4 = (bf16[256,128]{1,0:T(8,128)(2,1)}, bf16[256,128]{1,0:T(8,128)(2,1)S(1)}, u32[]{:S(2)}) copy-start(bf16[256,128]{1,0:T(8,128)(2,1)S(1)} %collective-permute-done.rest_1_) | copy-start | bytes 196612
  70.4 2.1 %copy-start.5 = (bf16[256,128]{1,0:T(8,128)(2,1)}, bf16[256,128]{1,0:T(8,128)(2,1)S(1)}, u32[]{:S(2)}) copy-start(bf16[256,128]{1,0:T(8,128)(2,1)S(1)} %collective-permute-done.1.rest_2_) | copy-start | bytes 196612
  72.5 0.6 copy-start.6
  83.2 4.8 %collective-permute-start.3 = (bf16[256,128]{1,0:T(8,128)(2,1)}, bf16[256,128]{1,0:T(8,128)(2,1)S(1)}, u32[]{:S(2)}, u32[]{:S(2)}) collective-permute-start(bf16[256,128]{1,0:T(8,128)(2,1)} %get-tuple-element.35), channel_id=1, source_target_pairs={{0,8},{8,0},{16,24},{24,16},{1,9},{9,1},{17,25},{25,17},{2,10},{10... | collective-permute-start | bytes 196616 | tf_op jit(solution)/shard_map/ppermute | solution.py:350
  83.2 5.4 %collective-permute-start.4 = (bf16[256,128]{1,0:T(8,128)(2,1)}, bf16[256,128]{1,0:T(8,128)(2,1)S(1)}, u32[]{:S(2)}, u32[]{:S(2)}) collective-permute-start(bf16[256,128]{1,0:T(8,128)(2,1)} %get-tuple-element.36), channel_id=1, source_target_pairs={{0,16},{8,24},{16,0},{24,8},{1,17},{9,25},{17,1},{25,9},{2,18},{10... | collective-permute-start | bytes 196616 | tf_op jit(solution)/shard_map/ppermute | solution.py:350
  84.9 6.3 %collective-permute-start.5 = (bf16[256,128]{1,0:T(8,128)(2,1)}, bf16[256,128]{1,0:T(8,128)(2,1)S(1)}, u32[]{:S(2)}, u32[]{:S(2)}) collective-permute-start(bf16[256,128]{1,0:T(8,128)(2,1)} %get-tuple-element.37), channel_id=1, source_target_pairs={{0,24},{8,16},{16,8},{24,0},{1,25},{9,17},{17,9},{25,1},{2,26},{10... | collective-permute-start | bytes 196616 | tf_op jit(solution)/shard_map/ppermute | solution.py:350
  88.0 3.2 %copy-start.7 = (bf16[256,128]{1,0:T(8,128)(2,1)}, bf16[256,128]{1,0:T(8,128)(2,1)S(1)}, u32[]{:S(2)}) copy-start(bf16[256,128]{1,0:T(8,128)(2,1)S(1)} %collective-permute-done.3.rest_1_) | copy-start | bytes 196612
  88.7 2.5 %copy-start.8 = (bf16[256,128]{1,0:T(8,128)(2,1)}, bf16[256,128]{1,0:T(8,128)(2,1)S(1)}, u32[]{:S(2)}) copy-start(bf16[256,128]{1,0:T(8,128)(2,1)S(1)} %collective-permute-done.4.rest_2_) | copy-start | bytes 196612
  91.1 0.6 copy-start.9
  94.5 13.6 %all-to-all-start.2 = ((bf16[8,256,128]{2,1,0:T(8,128)(2,1)}), bf16[8,256,128]{2,1,0:T(8,128)(2,1)S(1)}, u32[]{:S(2)}, u32[]{:S(2)}) async-start(bf16[8,256,128]{2,1,0:T(8,128)(2,1)} %width_back.1), calls=%async_computation.2 | async-start | bytes 1048576 | tf_op jit(solution)/shard_map/all_to_all | solution.py:760
  108.0 0.8 copy-start.3
  112.0 13.1 %all-to-all-start.3 = ((bf16[8,256,128]{2,1,0:T(8,128)(2,1)}), bf16[8,256,128]{2,1,0:T(8,128)(2,1)S(1)}, u32[]{:S(2)}, u32[]{:S(2)}) async-start(bf16[8,256,128]{2,1,0:T(8,128)(2,1)} %bitcast.19), calls=%async_computation.3 | async-start | bytes 1048576 | tf_op jit(solution)/shard_map/all_to_all | solution.py:764
  125.2 0.8 copy-start.1

commit v2 on v1

--- a/solution.py
+++ b/solution.py
@@ -49,6 +49,10 @@
 
 def vmem(count):
     return [pl.BlockSpec(memory_space=pltpu.VMEM) for _ in range(count)]
+
+
+def near(array):
+    return pltpu.with_memory_space_constraint(array, pltpu.MemorySpace.VMEM)
 
 
 def lane_left(shape, half):
@@ -100,8 +104,8 @@
         for group in range(cy // gj):
             dys = dy + group * gj * HALF
             start = (side * (cy // gj) + group) * rows
-            near = jnp.exp(-0.5 * (dxs * dxs + dys * dys + dz * dz)) * ROOT
-            near_ref[start : start + rows, :] = near
+            close = jnp.exp(-0.5 * (dxs * dxs + dys * dys + dz * dz)) * ROOT
+            near_ref[start : start + rows, :] = close
 
 
 def hidden(near_ref, base_ref, w_ref, h, cx, cy):
@@ -208,7 +212,7 @@
     cells = cx * cy
     rows = cells // 2
     count = out_weight.shape[0]
-    group = 8
+    group = ENCODE_GROUP
     smem = pl.BlockSpec(memory_space=pltpu.SMEM)
     full = lambda a: pl.BlockSpec(a.shape, lambda i: (0,) * a.ndim)
     payload = (ny, cap * rows + PLANE_ROWS, 2 * channels)
@@ -292,10 +296,10 @@
         out_specs=vmem(1)[0],
         out_shape=jax.ShapeDtypeStruct((M, rows, lanes), bf16),
         name="depth_forward",
-    )(got, *table_rows)
-
-
-def skip_body(cap, rows, width, got_ref, weight_ref, bias_ref, out_ref):
+    )(near(got), *table_rows)
+
+
+def skip_body(cap, rows, width, xr, got_ref, weight_ref, bias_ref, high_ref, low_ref, out_ref, back_high_ref, back_low_ref):
     lanes = got_ref.shape[2]
     weight = weight_ref[...]
     zero = jnp.zeros_like(weight)
@@ -306,6 +310,10 @@
     pair_low = (pair - pair_high.astype(f32)).astype(bf16)
     bias = jnp.concatenate([bias_ref[...], bias_ref[...]], 1)
     planes = got_ref[:, cap * rows :, :].reshape(-1, lanes)
+    onehot = plane_onehot(planes, cap, xr)
+    same = same_row(back_high_ref.shape, xr)
+    back_high_ref[...] = jnp.where(same, dot_rows(onehot, high_ref[...]), 0.0).astype(bf16)
+    back_low_ref[...] = jnp.where(same, dot_rows(onehot, low_ref[...]), 0.0).astype(bf16)
     onehot = plane_onehot(planes, cap, width)
     size = onehot.shape[0]
     same = same_row((size, size), width)
@@ -318,16 +326,17 @@
         out_ref[:, group * width : (group + 1) * width, :] = term.reshape(size // width, width, lanes)
 
 
-def skip(got, weight, bias, rows, cap, width):
+def skip(got, weight, bias, table_rows, rows, cap, width, xr):
     lanes = got.shape[2]
     slots = got.shape[0] * cap
-    return pl.pallas_call(
-        functools.partial(skip_body, cap, rows, width),
-        in_specs=vmem(3),
-        out_specs=vmem(1)[0],
-        out_shape=jax.ShapeDtypeStruct((slots, rows, lanes), f32),
+    back = jax.ShapeDtypeStruct((slots * xr, table_rows[0].shape[0]), bf16)
+    return pl.pallas_call(
+        functools.partial(skip_body, cap, rows, width, xr),
+        in_specs=vmem(5),
+        out_specs=vmem(3),
+        out_shape=[jax.ShapeDtypeStruct((slots, rows, lanes), f32), back, back],
         name="skip",
-    )(got, weight, bias)
+    )(got, weight, bias, *table_rows)
 
 
 def rows_of(ref, lead, start, size):
@@ -383,20 +392,24 @@
         out_shape=[jax.ShapeDtypeStruct((size // nx, lanes), bf16)] * nx,
         scratch_shapes=[pltpu.VMEM((size, lanes), f32)],
         name="width_forward",
-    )(me, data, *table)
-
-
-def mix_body(kb, nx, me_ref, *rest):
+    )(me, near(data), *table)
+
+
+def mix_body(kb, nx, inner, me_ref, *rest):
     in_refs = rest[:nx]
     spec_ref, forward_ref, high_ref, low_ref = rest[nx : nx + 4]
     out_refs = rest[nx + 4 : 2 * nx + 4]
-    pick_ref, right_ref, back_ref = rest[2 * nx + 4 :]
+    pick_ref, right_ref, back_ref, modes_ref, mixed_ref = rest[2 * nx + 4 :]
     lanes = in_refs[0].shape[1]
     channels = lanes // 2
     fold = MODE_ROWS // kb
     half = fold * channels
-
-    @pl.when(pl.program_id(0) == 0)
+    each = spec_ref.shape[1]
+    eb = right_ref.shape[0]
+    size = M * MODE_ROWS
+    step = pl.program_id(0)
+
+    @pl.when(step == 0)
     def _():
         shape = pick_ref.shape[1:]
         row = lax.broadcasted_iota(jnp.int32, shape, 0) % half
@@ -405,35 +418,31 @@
         wanted = wanted - 2 * fold * (lane // lanes)
         for v in range(pick_ref.shape[0]):
             pick_ref[v] = (wanted == 2 * fold * v * (shape[1] // lanes)).astype(f32).astype(bf16)
-
-    each = spec_ref.shape[1]
-    inner = in_refs[0].shape[0] // each
-    right = []
-    for e in range(each):
-        rows = slice(e * inner, (e + 1) * inner)
         for d in range(nx):
             start = pl.multiple_of(source(me_ref[0], d, nx) * inner, inner)
-            right_ref[e, pl.ds(start, inner), :] = in_refs[d][rows, :].astype(f32)
-        right.append(right_ref[e].astype(bf16))
-    right = jnp.concatenate(right, 1)
-    out = dot(forward_ref[...], jnp.concatenate([right, right], 0))
-    size = M * MODE_ROWS
-    left = lane_left((size, lanes), channels)
-    place = (lax.broadcasted_iota(jnp.int32, (size, lanes), 0) % MODE_ROWS) // kb
-    side = lax.broadcasted_iota(jnp.int32, (size, lanes), 1) // channels
-    masks = [place == 2 * pair + side for pair in range(fold // 2)]
-    modes = []
-    for e in range(each):
-        here = out[:, e * lanes : (e + 1) * lanes]
-        halves = jnp.where(left, here[:size], here[size:])
-        halves = halves + pltpu.roll(halves, channels, 1)
-        high = halves.astype(bf16).astype(f32)
-        low = halves - high
-        parts = [jnp.where(mask, part, 0.0) for part in (high, low) for mask in masks]
-        modes.append(jnp.concatenate(parts, 1).astype(bf16))
-    modes = jnp.concatenate(modes, 0)
+            piece = in_refs[d][...].astype(f32)
+            for e in range(eb):
+                right_ref[e, pl.ds(start, inner), :] = piece[e * inner : (e + 1) * inner]
+        left = lane_left((size, lanes), channels)
+        place = (lax.broadcasted_iota(jnp.int32, (size, lanes), 0) % MODE_ROWS) // kb
+        side = lax.broadcasted_iota(jnp.int32, (size, lanes), 1) // channels
+        masks = [place == 2 * pair + side for pair in range(fold // 2)]
+        for first in range(0, eb, each):
+            right = jnp.concatenate([right_ref[first + e].astype(bf16) for e in range(each)], 1)
+            out = dot(forward_ref[...], jnp.concatenate([right, right], 0))
+            for e in range(each):
+                here = out[:, e * lanes : (e + 1) * lanes]
+                halves = jnp.where(left, here[:size], here[size:])
+                halves = halves + pltpu.roll(halves, channels, 1)
+                high = halves.astype(bf16).astype(f32)
+                low = halves - high
+                parts = [jnp.where(mask, part, 0.0) for part in (high, low) for mask in masks]
+                modes = jnp.concatenate(parts, 1).astype(bf16)
+                modes_ref[first // each, e * size : (e + 1) * size, :] = modes
+
     totals = [jnp.zeros((M, MODE_ROWS, lanes), f32) for e in range(each)]
     width = pick_ref.shape[2] // lanes
+    modes = modes_ref[step]
     for v in range(pick_ref.shape[0]):
         spread = dot(modes, pick_ref[v])
         for w in range(width):
@@ -442,19 +451,26 @@
                 part = spread[e * size : (e + 1) * size, w * lanes : (w + 1) * lanes]
                 part = part.reshape(M, MODE_ROWS, lanes)
                 totals[e] = totals[e] + part * spec_ref[:, e, start : start + MODE_ROWS, :]
-    mixed = jnp.concatenate([total.reshape(size, lanes) for total in totals], 1)
-    high = mixed.astype(bf16)
-    low = (mixed - high.astype(f32)).astype(bf16)
-    back = dot(high_ref[...], high) + dot(high_ref[...], low) + dot(low_ref[...], high)
-    count = nx * inner
-    left = lane_left((count, lanes), channels)
-    for e in range(each):
-        here = back[:, e * lanes : (e + 1) * lanes]
-        here = here + pltpu.roll(here, channels, 1)
-        back_ref[e] = jnp.where(left, here[:count], here[count:])
+    mixed_ref[step] = jnp.concatenate([total.reshape(size, lanes) for total in totals], 1)
+
+    @pl.when(step == pl.num_programs(0) - 1)
+    def _():
+        count = nx * inner
+        left = lane_left((count, lanes), channels)
+        for group in range(eb // each):
+            mixed = mixed_ref[group]
+            high = mixed.astype(bf16)
+            low = (mixed - high.astype(f32)).astype(bf16)
+            back = dot(high_ref[...], high) + dot(high_ref[...], low) + dot(low_ref[...], high)
+            for e in range(each):
+                here = back[:, e * lanes : (e + 1) * lanes]
+                here = here + pltpu.roll(here, channels, 1)
+                back_ref[group * each + e] = jnp.where(left, here[:count], here[count:])
         for d in range(nx):
             start = pl.multiple_of(partner(me_ref[0], d, nx) * inner, inner)
-            out_refs[d][e * inner : (e + 1) * inner, :] = back_ref[e, pl.ds(start, inner), :].astype(bf16)
+            for e in range(eb):
+                made = back_ref[e, pl.ds(start, inner), :]
+                out_refs[d][e * inner : (e + 1) * inner, :] = made.astype(bf16)
 
 
 def mix(me, pieces, spec, forward, inverse, inner):
@@ -465,13 +481,14 @@
     spec = spec.reshape(M, eb, kb, chunks, lanes).transpose(0, 1, 3, 2, 4).reshape(M, eb, chunks * kb, lanes)
     full = lambda a: pl.BlockSpec(a.shape, lambda e: (0,) * a.ndim)
     each = 2 if eb % 2 == 0 else 1
-    piece = pl.BlockSpec((each * inner, lanes), lambda e: (e, 0))
+    piece = pl.BlockSpec((total, lanes), lambda e: (0, 0))
+    channels = lanes // 2
     fold = MODE_ROWS // kb
     return pl.pallas_call(
-        functools.partial(mix_body, kb, nx),
+        functools.partial(mix_body, kb, nx, inner),
         grid=(eb // each,),
         in_specs=[pl.BlockSpec(memory_space=pltpu.SMEM)]
-        + [piece] * nx
+        + vmem(nx)
         + [
             pl.BlockSpec((M, each) + spec.shape[2:], lambda e: (0, e, 0, 0)),
             full(forward),
@@ -482,11 +499,13 @@
         out_shape=[jax.ShapeDtypeStruct((total, lanes), bf16)] * nx,
         scratch_shapes=[
             pltpu.VMEM((chunks // fold // 2, fold * lanes, 2 * lanes), bf16),
-            pltpu.VMEM((each, nx * inner, lanes), f32),
-            pltpu.VMEM((each, nx * inner, lanes), f32),
+            pltpu.VMEM((eb, nx * inner, lanes), f32),
+            pltpu.VMEM((eb, nx * inner, lanes), f32),
+            pltpu.VMEM((eb // each, each * M * MODE_ROWS, 2 * fold * channels), bf16),
+            pltpu.VMEM((eb // each, M * MODE_ROWS, each * lanes), f32),
         ],
         name="mix",
-    )(me, *pieces, spec, forward, *inverse)
+    )(me, pieces[0], *[near(piece) for piece in pieces[1:]], spec, forward, *inverse)
 
 
 def width_back_body(kb, xr, nx, me_ref, *rest):
@@ -519,47 +538,36 @@
         out_shape=jax.ShapeDtypeStruct((ny, G // ny * inner, lanes), bf16),
         scratch_shapes=[pltpu.VMEM((M * inner, lanes), f32), pltpu.VMEM((G * inner, lanes), f32)],
         name="width_back",
-    )(me, *pieces, *table)
-
-
-def latent_body(cap, inner, xr, in_ref, planes_ref, skip_ref, high_ref, low_ref, out_ref, scratch):
+    )(me, pieces[0], *[near(piece) for piece in pieces[1:]], *table)
+
+
+def latent_body(inner, xr, in_ref, skip_ref, high_ref, low_ref, out_ref, scratch):
     ny, total, lanes = in_ref.shape
     slots = skip_ref.shape[0]
-    onehot = plane_onehot(planes_ref[...].reshape(-1, lanes), cap, xr)
-    shape = (onehot.shape[0], high_ref.shape[0])
-    same = same_row(shape, xr)
-    high = jnp.where(same, dot_rows(onehot, high_ref[...]), 0.0).astype(bf16)
-    low = jnp.where(same, dot_rows(onehot, low_ref[...]), 0.0).astype(bf16)
     for j in range(total // inner):
         right = jnp.concatenate([rows_of(in_ref, t, j * inner, inner) for t in range(ny)], 0).astype(bf16)
-        out = (dot(high, right) + dot(low, right)).reshape(slots, xr, lanes)
+        out = (dot(high_ref[...], right) + dot(low_ref[...], right)).reshape(slots, xr, lanes)
         here = slice(j * xr, (j + 1) * xr)
         out = out + skip_ref[:, here, :]
         scratch[:, here, :] = 0.5 * out * (1.0 + lax.erf(out * ROOT))
     out_ref[...] = scratch[...].astype(bf16)
 
 
-def latent_tiles(data, got, skipped, table_rows, cap, rows, inner, xr):
-    ny, _, lanes = data.shape
-    full = lambda a: pl.BlockSpec(a.shape, lambda i: (0,) * a.ndim)
-    return pl.pallas_call(
-        functools.partial(latent_body, cap, inner, xr),
-        grid=(1,),
-        in_specs=[
-            full(data),
-            pl.BlockSpec((ny, PLANE_ROWS, lanes), lambda i: (0, cap * rows // PLANE_ROWS, 0)),
-            full(skipped),
-            full(table_rows[0]),
-            full(table_rows[1]),
-        ],
-        out_specs=pl.BlockSpec(skipped.shape, lambda i: (0, 0, 0)),
+def latent_tiles(data, skipped, back, inner, xr):
+    return pl.pallas_call(
+        functools.partial(latent_body, inner, xr),
+        in_specs=vmem(4),
+        out_specs=vmem(1)[0],
         out_shape=jax.ShapeDtypeStruct(skipped.shape, bf16),
         scratch_shapes=[pltpu.VMEM(skipped.shape, f32)],
         name="latent",
-    )(data, got, skipped, *table_rows)
-
-
-STEP = 2
+    )(near(data), skipped, *back)
+
+
+STEP = 4
+DECODE_GROUP = 64
+AHEAD_GROUP = 16
+ENCODE_GROUP = 8
 
 
 def spread_body(out_w_ref, head_ref, wcol_ref, wide_ref):
@@ -614,7 +622,7 @@
     made = (blocks, count * cells, points)
     base_rows = count * max(8, cx // 2)
     return pl.pallas_call(
-        functools.partial(ahead_body, cx, cy, 16, first),
+        functools.partial(ahead_body, cx, cy, AHEAD_GROUP, first),
         grid=(number,),
         in_specs=[pl.BlockSpec(memory_space=pltpu.SMEM), full(weight_in), full(bias_in), full(offsets)]
         + [pl.BlockSpec(memory_space=pl.ANY)] * len(old),
@@ -632,17 +640,16 @@
 
 
 def decoder_body(cells, group, slot_ref, *rest):
-    tile_refs = rest[:STEP]
-    ready_ref, wcol_ref, wide_ref, out_ref = rest[STEP:]
+    tile_ref, ready_ref, wcol_ref, wide_ref, out_ref = rest
     step = pl.program_id(0)
     count, channels, _ = wcol_ref.shape
     points = ready_ref.shape[2]
 
     def tile_of(ref):
-        tile = ref[0].astype(f32).T
+        tile = ref[...].astype(f32).T
         return jnp.concatenate([tile[:channels], tile[channels:]], 1).astype(bf16)
 
-    tiles = [tile_of(ref) for ref in tile_refs]
+    tiles = [tile_of(tile_ref.at[slot_ref[STEP * step + q]]) for q in range(STEP)]
 
     def one(index, totals):
         first = index * group
@@ -664,19 +671,15 @@
 
 def decoder(slots, tiles, ready, wcol, wide, cells):
     blocks, _, points = ready.shape
-    group = 16
+    group = DECODE_GROUP
     full = lambda a: pl.BlockSpec(a.shape, lambda b, s: (0,) * a.ndim)
-    tile = (1,) + tiles.shape[1:]
-
-    def tile_spec(q):
-        return pl.BlockSpec(tile, lambda b, s: (s[STEP * b + q], 0, 0))
 
     return pl.pallas_call(
         functools.partial(decoder_body, cells, group),
         grid_spec=pltpu.PrefetchScalarGridSpec(
             num_scalar_prefetch=1,
             grid=(blocks // STEP,),
-            in_specs=[tile_spec(q) for q in range(STEP)]
+            in_specs=vmem(1)
             + [
                 pl.BlockSpec((STEP,) + ready.shape[1:], lambda b, s: (b, 0, 0)),
                 full(wcol),
@@ -686,7 +689,7 @@
         ),
         out_shape=jax.ShapeDtypeStruct((blocks, points), f32),
         name="decoder",
-    )(slots, *([tiles] * STEP), ready, wcol, wide)
+    )(slots, near(tiles), ready, wcol, wide)
 
 
 def local(
@@ -742,25 +745,26 @@
         targets[:, 0], zstart, enc_in, enc_bias[None, :], offs, point_feats, enc_out, cx, cy, ny, cap
     )
     third = blocks // 3
+    begin = blocks - 2 * third
     made = functools.partial(ahead, dec_in, dec_bias[None, :], offs, cx, cy)
     got = swap(payload, "gy")
-    ready = made(0, third, ())
+    ready = made(0, begin, ())
     got, ready = lax.optimization_barrier((got, ready))
     data = depth(got, depth_rows, rows, cap, 16)
-    ready = made(third, third, (ready,))
+    ready = made(begin, third, (ready,))
     data = swap(data.reshape(ny, kb * rows, lanes), "gy")
     data, ready = lax.optimization_barrier((data, ready))
     wcol, wide = spread(dec_out, head_weight[None, :], cx * cy, points)
-    skipped = skip(got, local_weight, local_bias[None, :], rows, cap, 16)
+    skipped, *back = skip(got, local_weight, local_bias[None, :], depth_back_rows, rows, cap, 16, xr)
     pieces = width_forward(me, data, width_table, nx, kb, xr)
     pieces = swap_pieces(pieces, "gx")
     pieces = mix(me, pieces, spec_weight, length_forward, length_back, inner)
     pieces = swap_pieces(pieces, "gx")
     data = width_back(me, pieces, width_back_table, ny, kb, xr)
     data = swap(data, "gy")
-    data, skipped, wcol, wide = lax.optimization_barrier((data, skipped, wcol, wide))
-    tiles = latent_tiles(data, got, skipped, depth_back_rows, cap, rows, inner, xr)
-    ready = made(2 * third, blocks - 2 * third, (ready,))
+    data, skipped, back, wcol, wide = lax.optimization_barrier((data, skipped, back, wcol, wide))
+    tiles = latent_tiles(data, skipped, back, inner, xr)
+    ready = made(begin + third, third, (ready,))
     tiles = swap(tiles.reshape(ny, cap * rows, lanes), "gy")
     tiles = tiles.reshape(ny * cap, rows, lanes)
     return decoder(slots, tiles, ready, wcol, wide, cx * cy)

time: 145 us -> 136 us (0.938)
  Pallas kernels: 99.6 us -> 94.4 us
  local copies, waits for them, and re-layouts: 4.48 us -> 0.01 us
    pallas_call x1, Pallas kernels: 18.3 us -> 13.8 us  [decoder(): pl.pallas_call(functools.partial(decoder_body, cells, group), grid_spec=p...]
    unnamed x20 -> x2, local copies, waits for them, and re-layouts: 4.48 us -> 0.01 us
  transfers between devices with their start and end apart: 10 -> 10, of which waited for: 10 -> 10; matrix products, arithmetic and copies ran while one was open for 0% -> 0% of each run, Pallas kernels for 23% -> 25%
where the time goes in v2:
time: 136 us; the launch traced here: 135 us
  Pallas kernels  94.4 us (69%)
  starting transfers between devices  24.9 us (18%)
  waiting for transfers between devices  15.3 us (11%)
    pallas_call x3, Pallas kernels, ahead(): pl.pallas_call(functools.partial(ahead_body, cx, cy, AHEAD_GROUP, first),...  26.4 us
    pallas_call x1, Pallas kernels, encoder(): pl.pallas_call(functools.partial(encoder_body, cx, cy, cap), grid=(blocks...  25.8 us
    pallas_call x1, Pallas kernels, decoder(): pl.pallas_call(functools.partial(decoder_body, cells, group), grid_spec=p...  13.8 us
    pallas_call x1, Pallas kernels, mix(): pl.pallas_call(functools.partial(mix_body, kb, nx, inner), grid=(eb // ea...  9.74 us
    ppermute x6, waiting for transfers between devices, swap_pieces(): moved.append(lax.ppermute(pieces[d], axis, pairs))  9.68 us
    ppermute x6, starting transfers between devices, swap_pieces(): moved.append(lax.ppermute(pieces[d], axis, pairs))  8.77 us
    all_to_all x1, starting transfers between devices, local(): got = swap(payload, 'gy')  5.22 us
    pallas_call x1, Pallas kernels, skip(): pl.pallas_call(functools.partial(skip_body, cap, rows, width, xr), in_spe...  4.86 us
  transfers between devices with their start and end apart: 10, of which 10 were waited for; matrix products, arithmetic and copies ran while one was open for 0% of the time, Pallas kernels for 25%

profile of v2, /device:TPU:0, one launch (start us, length us, event | category | flops | bytes accessed | tf_op | source)
XLA Modules:
  0.0 134.6 jit_solution(4569426187061669512)
XLA Ops:
  0.0 25.8 %encoder.1 = (bf16[8,272,128]{2,1,0:T(8,128)(2,1)}, s32[16]{0:T(128)}) custom-call(s32[16]{0:T(128)} %bitcast.26, s32[16]{0:T(128)} %z_ref.1, f32[3,64]{1,0:T(4,128)} %w_ref.4, f32[3,64]{1,0:T(4,128)} %w_ref.4, f32[1,64]{1,0:T(1,128)} %bitcast.27, bf16[3,16,128]{2,1,0:T(8,128)(2,1)} %bitcast.19, bf16[16,64,128]{2,1,0:T(8,128)(2,1)} %feats_ref.1, ...), custom_call_target="tpu_custom_call" | custom-call | tf_op jit(solution)/shard_map/encoder/pallas_call | solution.py:220
  25.8 5.2 %all-to-all-start = ((bf16[8,272,128]{2,1,0:T(8,128)(2,1)}), bf16[8,272,128]{2,1,0:T(8,128)(2,1)S(1)}, u32[]{:S(2)}, u32[]{:S(2)}) async-start(bf16[8,272,128]{2,1,0:T(8,128)(2,1)} %get-tuple-element.31), calls=%async_computation | async-start | bytes 1114112 | tf_op jit(solution)/shard_map/all_to_all | solution.py:750
  31.0 9.5 %ahead.3.rest_0_ = bf16[16,8192,128]{2,1,0:T(8,128)(2,1)} custom-call(f32[3,64]{1,0:T(4,128)} %w_ref.7, f32[3,64]{1,0:T(4,128)} %w_ref.7, f32[1,64]{1,0:T(1,128)} %bitcast.23, bf16[3,16,128]{2,1,0:T(8,128)(2,1)} %bitcast.20), custom_call_target="tpu_custom_call" | custom-call | tf_op jit(solution)/shard_map/ahead/pallas_call | solution.py:624
  40.5 0.5 all-to-all-done.got_ref
  41.1 0.0 copy-start
  41.1 3.6 %depth_forward.1 = bf16[32,64,128]{2,1,0:T(8,128)(2,1)} custom-call(bf16[8,272,128]{2,1,0:T(8,128)(2,1)S(1)} %all-to-all-done.got_ref, bf16[512,128]{1,0:T(8,128)(2,1)} %constant.27.clone.high_ref, bf16[512,128]{1,0:T(8,128)(2,1)} %constant.28.clone.low_ref), custom_call_target="tpu_custom_call" | custom-call | tf_op jit(solution)/shard_map/depth_forward/pallas_call | solution.py:293
  44.7 3.6 %all-to-all-start.1 = ((bf16[8,256,128]{2,1,0:T(8,128)(2,1)}), bf16[8,256,128]{2,1,0:T(8,128)(2,1)S(1)}, u32[]{:S(2)}, u32[]{:S(2)}) async-start(bf16[8,256,128]{2,1,0:T(8,128)(2,1)} %bitcast.17), calls=%async_computation.1 | async-start | bytes 1048576 | tf_op jit(solution)/shard_map/all_to_all | solution.py:755
  48.4 8.4 %ahead.4.rest_0_ = bf16[16,8192,128]{2,1,0:T(8,128)(2,1)} custom-call(f32[3,64]{1,0:T(4,128)} %w_ref.7, f32[3,64]{1,0:T(4,128)} %w_ref.7, f32[1,64]{1,0:T(1,128)} %bitcast.24, bf16[3,16,128]{2,1,0:T(8,128)(2,1)} %bitcast.21, bf16[16,8192,128]{2,1,0:T(8,128)(2,1)} %ahead.3.rest_0_), custom_call_target="tpu_custom_call", output_to_operand_aliasing={{}: (4, {})} | custom-call | tf_op jit(solution)/shard_map/ahead/pallas_call | solution.py:624
  56.8 0.0 copy-done
  56.8 1.3 all-to-all-done.1.in_ref
  58.1 2.4 %width_forward.1 = (bf16[256,128]{1,0:T(8,128)(2,1)}, bf16[256,128]{1,0:T(8,128)(2,1)}, bf16[256,128]{1,0:T(8,128)(2,1)}, bf16[256,128]{1,0:T(8,128)(2,1)}) custom-call(s32[1]{0:T(128)} %bitcast.3.me_ref, bf16[8,256,128]{2,1,0:T(8,128)(2,1)S(1)} %all-to-all-done.1.in_ref, bf16[256,512]{1,0:T(8,128)(2,1)} %constant.31.clone.high_ref, ...), custom_call_target="tpu_custom_call" | custom-call | tf_op jit(solution)/shard_map/width_forward/pallas_call | solution.py:388
  60.5 1.6 %collective-permute-start = (bf16[256,128]{1,0:T(8,128)(2,1)}, bf16[256,128]{1,0:T(8,128)(2,1)S(1)}, u32[]{:S(2)}, u32[]{:S(2)}) collective-permute-start(bf16[256,128]{1,0:T(8,128)(2,1)} %get-tuple-element.36), channel_id=1, source_target_pairs={{0,8},{8,0},{16,24},{24,16},{1,9},{9,1},{17,25},{25,17},{2,10},{10... | collective-permute-start | bytes 196616 | tf_op jit(solution)/shard_map/ppermute | solution.py:359
  62.1 2.6 %collective-permute-start.1 = (bf16[256,128]{1,0:T(8,128)(2,1)}, bf16[256,128]{1,0:T(8,128)(2,1)S(1)}, u32[]{:S(2)}, u32[]{:S(2)}) collective-permute-start(bf16[256,128]{1,0:T(8,128)(2,1)} %get-tuple-element.37), channel_id=1, source_target_pairs={{0,16},{8,24},{16,0},{24,8},{1,17},{9,25},{17,1},{25,9},{2,18},{10... | collective-permute-start | bytes 196616 | tf_op jit(solution)/shard_map/ppermute | solution.py:359
  64.7 0.2 collective-permute-start.2
  64.9 0.7 collective-permute-done.rest_1_
  65.6 3.3 %collective-permute-done.1.rest_2_ = bf16[256,128]{1,0:T(8,128)(2,1)S(1)} collective-permute-done((bf16[256,128]{1,0:T(8,128)(2,1)}, bf16[256,128]{1,0:T(8,128)(2,1)S(1)}, u32[]{:S(2)}, u32[]{:S(2)}) %collective-permute-start.1) | collective-permute-done | bytes 65568 | tf_op jit(solution)/shard_map/ppermute | solution.py:359
  68.9 2.0 %collective-permute-done.2.rest_3_ = bf16[256,128]{1,0:T(8,128)(2,1)S(1)} collective-permute-done((bf16[256,128]{1,0:T(8,128)(2,1)}, bf16[256,128]{1,0:T(8,128)(2,1)S(1)}, u32[]{:S(2)}, u32[]{:S(2)}) %collective-permute-start.2) | collective-permute-done | bytes 65568 | tf_op jit(solution)/shard_map/ppermute | solution.py:359
  71.0 9.7 %mix.1 = (bf16[256,128]{1,0:T(8,128)(2,1)}, bf16[256,128]{1,0:T(8,128)(2,1)}, bf16[256,128]{1,0:T(8,128)(2,1)}, bf16[256,128]{1,0:T(8,128)(2,1)}) custom-call(s32[1]{0:T(128)} %bitcast.3.me_ref, bf16[256,128]{1,0:T(8,128)(2,1)} %get-tuple-element.35.rest_0_, bf16[256,128]{1,0:T(8,128)(2,1)S(1)} %collective-permute-done.rest_1_, ...), custom_call_target="tpu_custom_call" | custom-call | tf_op jit(solution)/shard_map/mix/pallas_call | solution.py:487
  80.7 0.0 collective-permute-start.3
  80.7 1.7 %collective-permute-start.4 = (bf16[256,128]{1,0:T(8,128)(2,1)}, bf16[256,128]{1,0:T(8,128)(2,1)S(1)}, u32[]{:S(2)}, u32[]{:S(2)}) collective-permute-start(bf16[256,128]{1,0:T(8,128)(2,1)} %get-tuple-element.41), channel_id=1, source_target_pairs={{0,16},{8,24},{16,0},{24,8},{1,17},{9,25},{17,1},{25,9},{2,18},{10... | collective-permute-start | bytes 196616 | tf_op jit(solution)/shard_map/ppermute | solution.py:359
  82.4 2.6 %collective-permute-start.5 = (bf16[256,128]{1,0:T(8,128)(2,1)}, bf16[256,128]{1,0:T(8,128)(2,1)S(1)}, u32[]{:S(2)}, u32[]{:S(2)}) collective-permute-start(bf16[256,128]{1,0:T(8,128)(2,1)} %get-tuple-element.42), channel_id=1, source_target_pairs={{0,24},{8,16},{16,8},{24,0},{1,25},{9,17},{17,9},{25,1},{2,26},{10... | collective-permute-start | bytes 196616 | tf_op jit(solution)/shard_map/ppermute | solution.py:359
  85.1 0.4 collective-permute-done.3.rest_1_
  85.5 0.7 collective-permute-done.4.rest_2_
  86.1 2.6 %collective-permute-done.5.rest_3_ = bf16[256,128]{1,0:T(8,128)(2,1)S(1)} collective-permute-done((bf16[256,128]{1,0:T(8,128)(2,1)}, bf16[256,128]{1,0:T(8,128)(2,1)S(1)}, u32[]{:S(2)}, u32[]{:S(2)}) %collective-permute-start.5) | collective-permute-done | bytes 65568 | tf_op jit(solution)/shard_map/ppermute | solution.py:359
  88.7 2.6 %width_back.1 = bf16[8,256,128]{2,1,0:T(8,128)(2,1)} custom-call(s32[1]{0:T(128)} %bitcast.3.me_ref, bf16[256,128]{1,0:T(8,128)(2,1)} %get-tuple-element.39.rest_0_, bf16[256,128]{1,0:T(8,128)(2,1)S(1)} %collective-permute-done.3.rest_1_, bf16[256,128]{1,0:T(8,128)(2,1)S(1)} %collective-permute-done.4.rest_2_, ...), custom_call_target="tpu_custom_call" | custom-call | tf_op jit(solution)/shard_map/width_back/pallas_call | solution.py:534
  91.3 3.8 %all-to-all-start.2 = ((bf16[8,256,128]{2,1,0:T(8,128)(2,1)}), bf16[8,256,128]{2,1,0:T(8,128)(2,1)S(1)}, u32[]{:S(2)}, u32[]{:S(2)}) async-start(bf16[8,256,128]{2,1,0:T(8,128)(2,1)} %width_back.1), calls=%async_computation.2 | async-start | bytes 1048576 | tf_op jit(solution)/shard_map/all_to_all | solution.py:764
  95.1 2.3 %spread.1 = (bf16[64,64,128]{2,1,0:T(8,128)(2,1)}, f32[64,128]{1,0:T(8,128)}) custom-call(bf16[64,64]{1,0:T(8,128)(2,1)} %out_w_ref.3, f32[1,64]{1,0:T(1,128)} %bitcast.29), custom_call_target="tpu_custom_call" | custom-call | tf_op jit(solution)/shard_map/spread/pallas_call | solution.py:583
  97.4 4.9 %skip.1 = (f32[32,64,128]{2,1,0:T(8,128)}, bf16[256,256]{1,0:T(8,128)(2,1)}, bf16[256,256]{1,0:T(8,128)(2,1)}) custom-call(bf16[8,272,128]{2,1,0:T(8,128)(2,1)} %copy-done, f32[64,64]{1,0:T(8,128)} %weight_ref.1, f32[1,64]{1,0:T(1,128)} %bitcast.28, bf16[256,128]{1,0:T(8,128)(2,1)} %constant.29.clone.high_ref, bf16[256,128]{1,0:T(8,128)(2,1)} %constant.30.clone.low_ref), custom_call_target="tpu_custom_call" | custom-call | tf_op jit(solution)/shard_map/skip/pallas_call | solution.py:333
  102.3 2.6 %all-to-all-done.2.in_ref = bf16[8,256,128]{2,1,0:T(8,128)(2,1)S(1)} async-done(((bf16[8,256,128]{2,1,0:T(8,128)(2,1)}), bf16[8,256,128]{2,1,0:T(8,128)(2,1)S(1)}, u32[]{:S(2)}, u32[]{:S(2)}) %all-to-all-start.2) | async-done | bytes 524320 | tf_op jit(solution)/shard_map/all_to_all | solution.py:764
  104.8 2.8 %latent.1 = bf16[32,64,128]{2,1,0:T(8,128)(2,1)} custom-call(bf16[8,256,128]{2,1,0:T(8,128)(2,1)S(1)} %all-to-all-done.2.in_ref, f32[32,64,128]{2,1,0:T(8,128)} %get-tuple-element.49.skip_ref, bf16[256,256]{1,0:T(8,128)(2,1)} %get-tuple-element.50.high_ref, bf16[256,256]{1,0:T(8,128)(2,1)} %get-tuple-element.51.low_ref), custom_call_target="tpu_custom_call" | custom-call | tf_op jit(solution)/shard_map/latent/pallas_call | solution.py:557
  107.7 3.5 %all-to-all-start.3 = ((bf16[8,256,128]{2,1,0:T(8,128)(2,1)}), bf16[8,256,128]{2,1,0:T(8,128)(2,1)S(1)}, u32[]{:S(2)}, u32[]{:S(2)}) async-start(bf16[8,256,128]{2,1,0:T(8,128)(2,1)} %bitcast.18), calls=%async_computation.3 | async-start | bytes 1048576 | tf_op jit(solution)/shard_map/all_to_all | solution.py:768
  111.2 8.4 %ahead.5.rest_1_ = bf16[16,8192,128]{2,1,0:T(8,128)(2,1)} custom-call(f32[3,64]{1,0:T(4,128)} %w_ref.7, f32[3,64]{1,0:T(4,128)} %w_ref.7, f32[1,64]{1,0:T(1,128)} %bitcast.25, bf16[3,16,128]{2,1,0:T(8,128)(2,1)} %bitcast.22, bf16[16,8192,128]{2,1,0:T(8,128)(2,1)} %ahead.4.rest_0_), custom_call_target="tpu_custom_call", output_to_operand_aliasing={{}: (4, {})} | custom-call | tf_op jit(solution)/shard_map/ahead/pallas_call | solution.py:624
  119.6 1.2 all-to-all-done.3
  120.8 13.8 %decoder.1 = f32[16,128]{1,0:T(8,128)} custom-call(s32[16]{0:T(128)} %get-tuple-element.30.slot_ref, bf16[32,64,128]{2,1,0:T(8,128)(2,1)S(1)} %bitcast.15, bf16[16,8192,128]{2,1,0:T(8,128)(2,1)} %ahead.5.rest_1_, bf16[64,64,128]{2,1,0:T(8,128)(2,1)} %get-tuple-element.53.rest_2_, f32[64,128]{1,0:T(8,128)} %get-tuple-element.54.rest_3_), custom_call_target="tpu_custom_call" | custom-call | tf_op jit(solution)/shard_map/decoder/pallas_call | solution.py:677
Async XLA Ops:
  25.8 15.3 %all-to-all-start = ((bf16[8,272,128]{2,1,0:T(8,128)(2,1)}), bf16[8,272,128]{2,1,0:T(8,128)(2,1)S(1)}, u32[]{:S(2)}, u32[]{:S(2)}) async-start(bf16[8,272,128]{2,1,0:T(8,128)(2,1)} %get-tuple-element.31), calls=%async_computation | async-start | bytes 1114112 | tf_op jit(solution)/shard_map/all_to_all | solution.py:750
  41.1 15.7 %copy-start = (bf16[8,272,128]{2,1,0:T(8,128)(2,1)}, bf16[8,272,128]{2,1,0:T(8,128)(2,1)S(1)}, u32[]{:S(2)}) copy-start(bf16[8,272,128]{2,1,0:T(8,128)(2,1)S(1)} %all-to-all-done.got_ref) | copy-start | bytes 1671172
  44.7 13.3 %all-to-all-start.1 = ((bf16[8,256,128]{2,1,0:T(8,128)(2,1)}), bf16[8,256,128]{2,1,0:T(8,128)(2,1)S(1)}, u32[]{:S(2)}, u32[]{:S(2)}) async-start(bf16[8,256,128]{2,1,0:T(8,128)(2,1)} %bitcast.17), calls=%async_computation.1 | async-start | bytes 1048576 | tf_op jit(solution)/shard_map/all_to_all | solution.py:755
  60.5 5.1 %collective-permute-start = (bf16[256,128]{1,0:T(8,128)(2,1)}, bf16[256,128]{1,0:T(8,128)(2,1)S(1)}, u32[]{:S(2)}, u32[]{:S(2)}) collective-permute-start(bf16[256,128]{1,0:T(8,128)(2,1)} %get-tuple-element.36), channel_id=1, source_target_pairs={{0,8},{8,0},{16,24},{24,16},{1,9},{9,1},{17,25},{25,17},{2,10},{10... | collective-permute-start | bytes 196616 | tf_op jit(solution)/shard_map/ppermute | solution.py:359
  62.1 6.9 %collective-permute-start.1 = (bf16[256,128]{1,0:T(8,128)(2,1)}, bf16[256,128]{1,0:T(8,128)(2,1)S(1)}, u32[]{:S(2)}, u32[]{:S(2)}) collective-permute-start(bf16[256,128]{1,0:T(8,128)(2,1)} %get-tuple-element.37), channel_id=1, source_target_pairs={{0,16},{8,24},{16,0},{24,8},{1,17},{9,25},{17,1},{25,9},{2,18},{10... | collective-permute-start | bytes 196616 | tf_op jit(solution)/shard_map/ppermute | solution.py:359
  64.7 6.3 %collective-permute-start.2 = (bf16[256,128]{1,0:T(8,128)(2,1)}, bf16[256,128]{1,0:T(8,128)(2,1)S(1)}, u32[]{:S(2)}, u32[]{:S(2)}) collective-permute-start(bf16[256,128]{1,0:T(8,128)(2,1)} %get-tuple-element.38), channel_id=1, source_target_pairs={{0,24},{8,16},{16,8},{24,0},{1,25},{9,17},{17,9},{25,1},{2,26},{10... | collective-permute-start | bytes 196616 | tf_op jit(solution)/shard_map/ppermute | solution.py:359
  80.7 4.8 %collective-permute-start.3 = (bf16[256,128]{1,0:T(8,128)(2,1)}, bf16[256,128]{1,0:T(8,128)(2,1)S(1)}, u32[]{:S(2)}, u32[]{:S(2)}) collective-permute-start(bf16[256,128]{1,0:T(8,128)(2,1)} %get-tuple-element.40), channel_id=1, source_target_pairs={{0,8},{8,0},{16,24},{24,16},{1,9},{9,1},{17,25},{25,17},{2,10},{10... | collective-permute-start | bytes 196616 | tf_op jit(solution)/shard_map/ppermute | solution.py:359
  80.7 5.4 %collective-permute-start.4 = (bf16[256,128]{1,0:T(8,128)(2,1)}, bf16[256,128]{1,0:T(8,128)(2,1)S(1)}, u32[]{:S(2)}, u32[]{:S(2)}) collective-permute-start(bf16[256,128]{1,0:T(8,128)(2,1)} %get-tuple-element.41), channel_id=1, source_target_pairs={{0,16},{8,24},{16,0},{24,8},{1,17},{9,25},{17,1},{25,9},{2,18},{10... | collective-permute-start | bytes 196616 | tf_op jit(solution)/shard_map/ppermute | solution.py:359
  82.4 6.3 %collective-permute-start.5 = (bf16[256,128]{1,0:T(8,128)(2,1)}, bf16[256,128]{1,0:T(8,128)(2,1)S(1)}, u32[]{:S(2)}, u32[]{:S(2)}) collective-permute-start(bf16[256,128]{1,0:T(8,128)(2,1)} %get-tuple-element.42), channel_id=1, source_target_pairs={{0,24},{8,16},{16,8},{24,0},{1,25},{9,17},{17,9},{25,1},{2,26},{10... | collective-permute-start | bytes 196616 | tf_op jit(solution)/shard_map/ppermute | solution.py:359
  91.3 13.5 %all-to-all-start.2 = ((bf16[8,256,128]{2,1,0:T(8,128)(2,1)}), bf16[8,256,128]{2,1,0:T(8,128)(2,1)S(1)}, u32[]{:S(2)}, u32[]{:S(2)}) async-start(bf16[8,256,128]{2,1,0:T(8,128)(2,1)} %width_back.1), calls=%async_computation.2 | async-start | bytes 1048576 | tf_op jit(solution)/shard_map/all_to_all | solution.py:764
  107.7 13.1 %all-to-all-start.3 = ((bf16[8,256,128]{2,1,0:T(8,128)(2,1)}), bf16[8,256,128]{2,1,0:T(8,128)(2,1)S(1)}, u32[]{:S(2)}, u32[]{:S(2)}) async-start(bf16[8,256,128]{2,1,0:T(8,128)(2,1)} %bitcast.18), calls=%async_computation.3 | async-start | bytes 1048576 | tf_op jit(solution)/shard_map/all_to_all | solution.py:768

commit v3 on v2

--- a/solution.py
+++ b/solution.py
@@ -273,6 +273,10 @@
     return jnp.concatenate(parts, 0)
 
 
+def paired(count):
+    return 2 if count % 2 == 0 else 1
+
+
 def depth_body(cap, rows, width, got_ref, high_ref, low_ref, out_ref):
     lanes = got_ref.shape[2]
     planes = got_ref[:, cap * rows :, :].reshape(-1, lanes)
@@ -282,10 +286,14 @@
     high = jnp.where(same, dot_rows(high_ref[...], onehot), 0.0).astype(bf16)
     low = jnp.where(same, dot_rows(low_ref[...], onehot), 0.0).astype(bf16)
     modes = out_ref.shape[0]
-    for group in range(rows // width):
-        right = slot_rows(got_ref, cap, rows, group, width)
-        out = dot(high, right) + dot(low, right)
-        out_ref[:, group * width : (group + 1) * width, :] = out.astype(bf16).reshape(modes, width, lanes)
+    pair = paired(rows // width)
+    for first in range(0, rows // width, pair):
+        groups = range(first, first + pair)
+        right = jnp.concatenate([slot_rows(got_ref, cap, rows, group, width) for group in groups], 1)
+        out = (dot(high, right) + dot(low, right)).astype(bf16)
+        for group in groups:
+            part = out[:, (group - first) * lanes : (group - first + 1) * lanes]
+            out_ref[:, group * width : (group + 1) * width, :] = part.reshape(modes, width, lanes)
 
 
 def depth(got, table_rows, rows, cap, width):
@@ -371,11 +379,21 @@
     ny, total, lanes = in_ref.shape
     rows = total // kb
     inner = kb * xr
-    for k in range(kb):
-        right = jnp.concatenate([in_ref[y, k * rows : (k + 1) * rows, :] for y in range(ny)], 0)
+    pair = paired(kb)
+    for first in range(0, kb, pair):
+        ks = range(first, first + pair)
+        right = jnp.concatenate(
+            [
+                jnp.concatenate([in_ref[y, k * rows : (k + 1) * rows, :] for k in ks], 1)
+                for y in range(ny)
+            ],
+            0,
+        )
         out = dot(high_ref[...], right) + dot(low_ref[...], right)
-        for e in range(M):
-            scratch[e * inner + k * xr : e * inner + (k + 1) * xr, :] = out[e * xr : (e + 1) * xr]
+        for k in ks:
+            part = out[:, (k - first) * lanes : (k - first + 1) * lanes]
+            for e in range(M):
+                scratch[e * inner + k * xr : e * inner + (k + 1) * xr, :] = part[e * xr : (e + 1) * xr]
     size = M * inner // nx
     for d in range(nx):
         start = pl.multiple_of(partner(me_ref[0], d, nx) * size, size)
@@ -517,13 +535,23 @@
     for d in range(nx):
         start = pl.multiple_of(source(me_ref[0], d, nx) * total, total)
         right_ref[pl.ds(start, total), :] = in_refs[d][...].astype(f32)
-    for k in range(kb):
+    pair = paired(kb)
+    for first in range(0, kb, pair):
+        ks = range(first, first + pair)
         right = jnp.concatenate(
-            [right_ref[e * inner + k * xr : e * inner + (k + 1) * xr, :] for e in range(M)], 0
-        ).astype(bf16)
+            [
+                jnp.concatenate(
+                    [right_ref[e * inner + k * xr : e * inner + (k + 1) * xr, :] for e in range(M)], 0
+                ).astype(bf16)
+                for k in ks
+            ],
+            1,
+        )
         out = dot(high_ref[...], right) + dot(low_ref[...], right)
-        for y in range(G):
-            made_ref[y * inner + k * xr : y * inner + (k + 1) * xr, :] = out[y * xr : (y + 1) * xr]
+        for k in ks:
+            part = out[:, (k - first) * lanes : (k - first + 1) * lanes]
+            for y in range(G):
+                made_ref[y * inner + k * xr : y * inner + (k + 1) * xr, :] = part[y * xr : (y + 1) * xr]
     out_ref[...] = made_ref[...].astype(bf16).reshape(out_ref.shape)
 
 
@@ -544,12 +572,22 @@
 def latent_body(inner, xr, in_ref, skip_ref, high_ref, low_ref, out_ref, scratch):
     ny, total, lanes = in_ref.shape
     slots = skip_ref.shape[0]
-    for j in range(total // inner):
-        right = jnp.concatenate([rows_of(in_ref, t, j * inner, inner) for t in range(ny)], 0).astype(bf16)
-        out = (dot(high_ref[...], right) + dot(low_ref[...], right)).reshape(slots, xr, lanes)
-        here = slice(j * xr, (j + 1) * xr)
-        out = out + skip_ref[:, here, :]
-        scratch[:, here, :] = 0.5 * out * (1.0 + lax.erf(out * ROOT))
+    pair = paired(total // inner)
+    for first in range(0, total // inner, pair):
+        js = range(first, first + pair)
+        right = jnp.concatenate(
+            [
+                jnp.concatenate([rows_of(in_ref, t, j * inner, inner) for t in range(ny)], 0).astype(bf16)
+                for j in js
+            ],
+            1,
+        )
+        both = dot(high_ref[...], right) + dot(low_ref[...], right)
+        for j in js:
+            out = both[:, (j - first) * lanes : (j - first + 1) * lanes].reshape(slots, xr, lanes)
+            here = slice(j * xr, (j + 1) * xr)
+            out = out + skip_ref[:, here, :]
+            scratch[:, here, :] = 0.5 * out * (1.0 + lax.erf(out * ROOT))
     out_ref[...] = scratch[...].astype(bf16)
 
 

time: 136 us -> 134 us (0.985)
  no operation moved by 1% of the time
where the time goes in v3:
time: 134 us; the launch traced here: 133 us
  Pallas kernels  93.1 us (69%)
  starting transfers between devices  24.9 us (19%)
  waiting for transfers between devices  15.3 us (11%)
    pallas_call x3, Pallas kernels, ahead(): pl.pallas_call(functools.partial(ahead_body, cx, cy, AHEAD_GROUP, first),...  26.4 us
    pallas_call x1, Pallas kernels, encoder(): pl.pallas_call(functools.partial(encoder_body, cx, cy, cap), grid=(blocks...  25.8 us
    pallas_call x1, Pallas kernels, decoder(): pl.pallas_call(functools.partial(decoder_body, cells, group), grid_spec=p...  13.8 us
    pallas_call x1, Pallas kernels, mix(): pl.pallas_call(functools.partial(mix_body, kb, nx, inner), grid=(eb // ea...  9.73 us
    ppermute x6, waiting for transfers between devices, swap_pieces(): moved.append(lax.ppermute(pieces[d], axis, pairs))  9.7 us
    ppermute x6, starting transfers between devices, swap_pieces(): moved.append(lax.ppermute(pieces[d], axis, pairs))  8.77 us
    all_to_all x1, starting transfers between devices, local(): got = swap(payload, 'gy')  5.22 us
    pallas_call x1, Pallas kernels, skip(): pl.pallas_call(functools.partial(skip_body, cap, rows, width, xr), in_spe...  4.85 us
  transfers between devices with their start and end apart: 10, of which 10 were waited for; matrix products, arithmetic and copies ran while one was open for 0% of the time, Pallas kernels for 25%

profile of v3, /device:TPU:0, one launch (start us, length us, event | category | flops | bytes accessed | tf_op | source)
XLA Modules:
  0.0 133.4 jit_solution(6350270177695632735)
XLA Ops:
  0.0 25.8 %encoder.1 = (bf16[8,272,128]{2,1,0:T(8,128)(2,1)}, s32[16]{0:T(128)}) custom-call(s32[16]{0:T(128)} %bitcast.26, s32[16]{0:T(128)} %z_ref.1, f32[3,64]{1,0:T(4,128)} %w_ref.4, f32[3,64]{1,0:T(4,128)} %w_ref.4, f32[1,64]{1,0:T(1,128)} %bitcast.27, bf16[3,16,128]{2,1,0:T(8,128)(2,1)} %bitcast.19, bf16[16,64,128]{2,1,0:T(8,128)(2,1)} %feats_ref.1, ...), custom_call_target="tpu_custom_call" | custom-call | tf_op jit(solution)/shard_map/encoder/pallas_call | solution.py:220
  25.8 5.2 %all-to-all-start = ((bf16[8,272,128]{2,1,0:T(8,128)(2,1)}), bf16[8,272,128]{2,1,0:T(8,128)(2,1)S(1)}, u32[]{:S(2)}, u32[]{:S(2)}) async-start(bf16[8,272,128]{2,1,0:T(8,128)(2,1)} %get-tuple-element.31), calls=%async_computation | async-start | bytes 1114112 | tf_op jit(solution)/shard_map/all_to_all | solution.py:788
  31.0 9.5 %ahead.3.rest_0_ = bf16[16,8192,128]{2,1,0:T(8,128)(2,1)} custom-call(f32[3,64]{1,0:T(4,128)} %w_ref.7, f32[3,64]{1,0:T(4,128)} %w_ref.7, f32[1,64]{1,0:T(1,128)} %bitcast.23, bf16[3,16,128]{2,1,0:T(8,128)(2,1)} %bitcast.20), custom_call_target="tpu_custom_call" | custom-call | tf_op jit(solution)/shard_map/ahead/pallas_call | solution.py:662
  40.5 0.5 all-to-all-done.got_ref
  41.1 0.0 copy-start
  41.1 3.1 %depth_forward.1 = bf16[32,64,128]{2,1,0:T(8,128)(2,1)} custom-call(bf16[8,272,128]{2,1,0:T(8,128)(2,1)S(1)} %all-to-all-done.got_ref, bf16[512,128]{1,0:T(8,128)(2,1)} %constant.27.clone.high_ref, bf16[512,128]{1,0:T(8,128)(2,1)} %constant.28.clone.low_ref), custom_call_target="tpu_custom_call" | custom-call | tf_op jit(solution)/shard_map/depth_forward/pallas_call | solution.py:301
  44.2 3.6 %all-to-all-start.1 = ((bf16[8,256,128]{2,1,0:T(8,128)(2,1)}), bf16[8,256,128]{2,1,0:T(8,128)(2,1)S(1)}, u32[]{:S(2)}, u32[]{:S(2)}) async-start(bf16[8,256,128]{2,1,0:T(8,128)(2,1)} %bitcast.17), calls=%async_computation.1 | async-start | bytes 1048576 | tf_op jit(solution)/shard_map/all_to_all | solution.py:793
  47.8 8.4 %ahead.4.rest_0_ = bf16[16,8192,128]{2,1,0:T(8,128)(2,1)} custom-call(f32[3,64]{1,0:T(4,128)} %w_ref.7, f32[3,64]{1,0:T(4,128)} %w_ref.7, f32[1,64]{1,0:T(1,128)} %bitcast.24, bf16[3,16,128]{2,1,0:T(8,128)(2,1)} %bitcast.21, bf16[16,8192,128]{2,1,0:T(8,128)(2,1)} %ahead.3.rest_0_), custom_call_target="tpu_custom_call", output_to_operand_aliasing={{}: (4, {})} | custom-call | tf_op jit(solution)/shard_map/ahead/pallas_call | solution.py:662
  56.3 0.0 copy-done
  56.3 1.3 all-to-all-done.1.in_ref
  57.5 2.2 %width_forward.1 = (bf16[256,128]{1,0:T(8,128)(2,1)}, bf16[256,128]{1,0:T(8,128)(2,1)}, bf16[256,128]{1,0:T(8,128)(2,1)}, bf16[256,128]{1,0:T(8,128)(2,1)}) custom-call(s32[1]{0:T(128)} %bitcast.3.me_ref, bf16[8,256,128]{2,1,0:T(8,128)(2,1)S(1)} %all-to-all-done.1.in_ref, bf16[256,512]{1,0:T(8,128)(2,1)} %constant.31.clone.high_ref, ...), custom_call_target="tpu_custom_call" | custom-call | tf_op jit(solution)/shard_map/width_forward/pallas_call | solution.py:406
  59.7 1.6 %collective-permute-start = (bf16[256,128]{1,0:T(8,128)(2,1)}, bf16[256,128]{1,0:T(8,128)(2,1)S(1)}, u32[]{:S(2)}, u32[]{:S(2)}) collective-permute-start(bf16[256,128]{1,0:T(8,128)(2,1)} %get-tuple-element.36), channel_id=1, source_target_pairs={{0,8},{8,0},{16,24},{24,16},{1,9},{9,1},{17,25},{25,17},{2,10},{10... | collective-permute-start | bytes 196616 | tf_op jit(solution)/shard_map/ppermute | solution.py:367
  61.3 2.6 %collective-permute-start.1 = (bf16[256,128]{1,0:T(8,128)(2,1)}, bf16[256,128]{1,0:T(8,128)(2,1)S(1)}, u32[]{:S(2)}, u32[]{:S(2)}) collective-permute-start(bf16[256,128]{1,0:T(8,128)(2,1)} %get-tuple-element.37), channel_id=1, source_target_pairs={{0,16},{8,24},{16,0},{24,8},{1,17},{9,25},{17,1},{25,9},{2,18},{10... | collective-permute-start | bytes 196616 | tf_op jit(solution)/shard_map/ppermute | solution.py:367
  63.9 0.2 collective-permute-start.2
  64.1 0.7 collective-permute-done.rest_1_
  64.8 3.3 %collective-permute-done.1.rest_2_ = bf16[256,128]{1,0:T(8,128)(2,1)S(1)} collective-permute-done((bf16[256,128]{1,0:T(8,128)(2,1)}, bf16[256,128]{1,0:T(8,128)(2,1)S(1)}, u32[]{:S(2)}, u32[]{:S(2)}) %collective-permute-start.1) | collective-permute-done | bytes 65568 | tf_op jit(solution)/shard_map/ppermute | solution.py:367
  68.2 2.0 %collective-permute-done.2.rest_3_ = bf16[256,128]{1,0:T(8,128)(2,1)S(1)} collective-permute-done((bf16[256,128]{1,0:T(8,128)(2,1)}, bf16[256,128]{1,0:T(8,128)(2,1)S(1)}, u32[]{:S(2)}, u32[]{:S(2)}) %collective-permute-start.2) | collective-permute-done | bytes 65568 | tf_op jit(solution)/shard_map/ppermute | solution.py:367
  70.2 9.7 %mix.1 = (bf16[256,128]{1,0:T(8,128)(2,1)}, bf16[256,128]{1,0:T(8,128)(2,1)}, bf16[256,128]{1,0:T(8,128)(2,1)}, bf16[256,128]{1,0:T(8,128)(2,1)}) custom-call(s32[1]{0:T(128)} %bitcast.3.me_ref, bf16[256,128]{1,0:T(8,128)(2,1)} %get-tuple-element.35.rest_0_, bf16[256,128]{1,0:T(8,128)(2,1)S(1)} %collective-permute-done.rest_1_, ...), custom_call_target="tpu_custom_call" | custom-call | tf_op jit(solution)/shard_map/mix/pallas_call | solution.py:505
  79.9 0.0 collective-permute-start.3
  79.9 1.8 %collective-permute-start.4 = (bf16[256,128]{1,0:T(8,128)(2,1)}, bf16[256,128]{1,0:T(8,128)(2,1)S(1)}, u32[]{:S(2)}, u32[]{:S(2)}) collective-permute-start(bf16[256,128]{1,0:T(8,128)(2,1)} %get-tuple-element.41), channel_id=1, source_target_pairs={{0,16},{8,24},{16,0},{24,8},{1,17},{9,25},{17,1},{25,9},{2,18},{10... | collective-permute-start | bytes 196616 | tf_op jit(solution)/shard_map/ppermute | solution.py:367
  81.6 2.6 %collective-permute-start.5 = (bf16[256,128]{1,0:T(8,128)(2,1)}, bf16[256,128]{1,0:T(8,128)(2,1)S(1)}, u32[]{:S(2)}, u32[]{:S(2)}) collective-permute-start(bf16[256,128]{1,0:T(8,128)(2,1)} %get-tuple-element.42), channel_id=1, source_target_pairs={{0,24},{8,16},{16,8},{24,0},{1,25},{9,17},{17,9},{25,1},{2,26},{10... | collective-permute-start | bytes 196616 | tf_op jit(solution)/shard_map/ppermute | solution.py:367
  84.3 0.4 collective-permute-done.3.rest_1_
  84.7 0.7 collective-permute-done.4.rest_2_
  85.4 2.6 %collective-permute-done.5.rest_3_ = bf16[256,128]{1,0:T(8,128)(2,1)S(1)} collective-permute-done((bf16[256,128]{1,0:T(8,128)(2,1)}, bf16[256,128]{1,0:T(8,128)(2,1)S(1)}, u32[]{:S(2)}, u32[]{:S(2)}) %collective-permute-start.5) | collective-permute-done | bytes 65568 | tf_op jit(solution)/shard_map/ppermute | solution.py:367
  87.9 2.3 %width_back.1 = bf16[8,256,128]{2,1,0:T(8,128)(2,1)} custom-call(s32[1]{0:T(128)} %bitcast.3.me_ref, bf16[256,128]{1,0:T(8,128)(2,1)} %get-tuple-element.39.rest_0_, bf16[256,128]{1,0:T(8,128)(2,1)S(1)} %collective-permute-done.3.rest_1_, bf16[256,128]{1,0:T(8,128)(2,1)S(1)} %collective-permute-done.4.rest_2_, ...), custom_call_target="tpu_custom_call" | custom-call | tf_op jit(solution)/shard_map/width_back/pallas_call | solution.py:562
  90.3 3.8 %all-to-all-start.2 = ((bf16[8,256,128]{2,1,0:T(8,128)(2,1)}), bf16[8,256,128]{2,1,0:T(8,128)(2,1)S(1)}, u32[]{:S(2)}, u32[]{:S(2)}) async-start(bf16[8,256,128]{2,1,0:T(8,128)(2,1)} %width_back.1), calls=%async_computation.2 | async-start | bytes 1048576 | tf_op jit(solution)/shard_map/all_to_all | solution.py:802
  94.1 2.3 %spread.1 = (bf16[64,64,128]{2,1,0:T(8,128)(2,1)}, f32[64,128]{1,0:T(8,128)}) custom-call(bf16[64,64]{1,0:T(8,128)(2,1)} %out_w_ref.3, f32[1,64]{1,0:T(1,128)} %bitcast.29), custom_call_target="tpu_custom_call" | custom-call | tf_op jit(solution)/shard_map/spread/pallas_call | solution.py:621
  96.3 4.8 %skip.1 = (f32[32,64,128]{2,1,0:T(8,128)}, bf16[256,256]{1,0:T(8,128)(2,1)}, bf16[256,256]{1,0:T(8,128)(2,1)}) custom-call(bf16[8,272,128]{2,1,0:T(8,128)(2,1)} %copy-done, f32[64,64]{1,0:T(8,128)} %weight_ref.1, f32[1,64]{1,0:T(1,128)} %bitcast.28, bf16[256,128]{1,0:T(8,128)(2,1)} %constant.29.clone.high_ref, bf16[256,128]{1,0:T(8,128)(2,1)} %constant.30.clone.low_ref), custom_call_target="tpu_custom_call" | custom-call | tf_op jit(solution)/shard_map/skip/pallas_call | solution.py:341
  101.2 2.6 %all-to-all-done.2.in_ref = bf16[8,256,128]{2,1,0:T(8,128)(2,1)S(1)} async-done(((bf16[8,256,128]{2,1,0:T(8,128)(2,1)}), bf16[8,256,128]{2,1,0:T(8,128)(2,1)S(1)}, u32[]{:S(2)}, u32[]{:S(2)}) %all-to-all-start.2) | async-done | bytes 524320 | tf_op jit(solution)/shard_map/all_to_all | solution.py:802
  103.8 2.6 %latent.1 = bf16[32,64,128]{2,1,0:T(8,128)(2,1)} custom-call(bf16[8,256,128]{2,1,0:T(8,128)(2,1)S(1)} %all-to-all-done.2.in_ref, f32[32,64,128]{2,1,0:T(8,128)} %get-tuple-element.49.skip_ref, bf16[256,256]{1,0:T(8,128)(2,1)} %get-tuple-element.50.high_ref, bf16[256,256]{1,0:T(8,128)(2,1)} %get-tuple-element.51.low_ref), custom_call_target="tpu_custom_call" | custom-call | tf_op jit(solution)/shard_map/latent/pallas_call | solution.py:595
  106.4 3.5 %all-to-all-start.3 = ((bf16[8,256,128]{2,1,0:T(8,128)(2,1)}), bf16[8,256,128]{2,1,0:T(8,128)(2,1)S(1)}, u32[]{:S(2)}, u32[]{:S(2)}) async-start(bf16[8,256,128]{2,1,0:T(8,128)(2,1)} %bitcast.18), calls=%async_computation.3 | async-start | bytes 1048576 | tf_op jit(solution)/shard_map/all_to_all | solution.py:806
  109.9 8.4 %ahead.5.rest_1_ = bf16[16,8192,128]{2,1,0:T(8,128)(2,1)} custom-call(f32[3,64]{1,0:T(4,128)} %w_ref.7, f32[3,64]{1,0:T(4,128)} %w_ref.7, f32[1,64]{1,0:T(1,128)} %bitcast.25, bf16[3,16,128]{2,1,0:T(8,128)(2,1)} %bitcast.22, bf16[16,8192,128]{2,1,0:T(8,128)(2,1)} %ahead.4.rest_0_), custom_call_target="tpu_custom_call", output_to_operand_aliasing={{}: (4, {})} | custom-call | tf_op jit(solution)/shard_map/ahead/pallas_call | solution.py:662
  118.3 1.2 all-to-all-done.3
  119.5 13.8 %decoder.1 = f32[16,128]{1,0:T(8,128)} custom-call(s32[16]{0:T(128)} %get-tuple-element.30.slot_ref, bf16[32,64,128]{2,1,0:T(8,128)(2,1)S(1)} %bitcast.15, bf16[16,8192,128]{2,1,0:T(8,128)(2,1)} %ahead.5.rest_1_, bf16[64,64,128]{2,1,0:T(8,128)(2,1)} %get-tuple-element.53.rest_2_, f32[64,128]{1,0:T(8,128)} %get-tuple-element.54.rest_3_), custom_call_target="tpu_custom_call" | custom-call | tf_op jit(solution)/shard_map/decoder/pallas_call | solution.py:715
Async XLA Ops:
  25.8 15.3 %all-to-all-start = ((bf16[8,272,128]{2,1,0:T(8,128)(2,1)}), bf16[8,272,128]{2,1,0:T(8,128)(2,1)S(1)}, u32[]{:S(2)}, u32[]{:S(2)}) async-start(bf16[8,272,128]{2,1,0:T(8,128)(2,1)} %get-tuple-element.31), calls=%async_computation | async-start | bytes 1114112 | tf_op jit(solution)/shard_map/all_to_all | solution.py:788
  41.1 15.2 %copy-start = (bf16[8,272,128]{2,1,0:T(8,128)(2,1)}, bf16[8,272,128]{2,1,0:T(8,128)(2,1)S(1)}, u32[]{:S(2)}) copy-start(bf16[8,272,128]{2,1,0:T(8,128)(2,1)S(1)} %all-to-all-done.got_ref) | copy-start | bytes 1671172
  44.2 13.4 %all-to-all-start.1 = ((bf16[8,256,128]{2,1,0:T(8,128)(2,1)}), bf16[8,256,128]{2,1,0:T(8,128)(2,1)S(1)}, u32[]{:S(2)}, u32[]{:S(2)}) async-start(bf16[8,256,128]{2,1,0:T(8,128)(2,1)} %bitcast.17), calls=%async_computation.1 | async-start | bytes 1048576 | tf_op jit(solution)/shard_map/all_to_all | solution.py:793
  59.7 5.1 %collective-permute-start = (bf16[256,128]{1,0:T(8,128)(2,1)}, bf16[256,128]{1,0:T(8,128)(2,1)S(1)}, u32[]{:S(2)}, u32[]{:S(2)}) collective-permute-start(bf16[256,128]{1,0:T(8,128)(2,1)} %get-tuple-element.36), channel_id=1, source_target_pairs={{0,8},{8,0},{16,24},{24,16},{1,9},{9,1},{17,25},{25,17},{2,10},{10... | collective-permute-start | bytes 196616 | tf_op jit(solution)/shard_map/ppermute | solution.py:367
  61.3 6.9 %collective-permute-start.1 = (bf16[256,128]{1,0:T(8,128)(2,1)}, bf16[256,128]{1,0:T(8,128)(2,1)S(1)}, u32[]{:S(2)}, u32[]{:S(2)}) collective-permute-start(bf16[256,128]{1,0:T(8,128)(2,1)} %get-tuple-element.37), channel_id=1, source_target_pairs={{0,16},{8,24},{16,0},{24,8},{1,17},{9,25},{17,1},{25,9},{2,18},{10... | collective-permute-start | bytes 196616 | tf_op jit(solution)/shard_map/ppermute | solution.py:367
  63.9 6.3 %collective-permute-start.2 = (bf16[256,128]{1,0:T(8,128)(2,1)}, bf16[256,128]{1,0:T(8,128)(2,1)S(1)}, u32[]{:S(2)}, u32[]{:S(2)}) collective-permute-start(bf16[256,128]{1,0:T(8,128)(2,1)} %get-tuple-element.38), channel_id=1, source_target_pairs={{0,24},{8,16},{16,8},{24,0},{1,25},{9,17},{17,9},{25,1},{2,26},{10... | collective-permute-start | bytes 196616 | tf_op jit(solution)/shard_map/ppermute | solution.py:367
  79.9 4.8 %collective-permute-start.3 = (bf16[256,128]{1,0:T(8,128)(2,1)}, bf16[256,128]{1,0:T(8,128)(2,1)S(1)}, u32[]{:S(2)}, u32[]{:S(2)}) collective-permute-start(bf16[256,128]{1,0:T(8,128)(2,1)} %get-tuple-element.40), channel_id=1, source_target_pairs={{0,8},{8,0},{16,24},{24,16},{1,9},{9,1},{17,25},{25,17},{2,10},{10... | collective-permute-start | bytes 196616 | tf_op jit(solution)/shard_map/ppermute | solution.py:367
  79.9 5.5 %collective-permute-start.4 = (bf16[256,128]{1,0:T(8,128)(2,1)}, bf16[256,128]{1,0:T(8,128)(2,1)S(1)}, u32[]{:S(2)}, u32[]{:S(2)}) collective-permute-start(bf16[256,128]{1,0:T(8,128)(2,1)} %get-tuple-element.41), channel_id=1, source_target_pairs={{0,16},{8,24},{16,0},{24,8},{1,17},{9,25},{17,1},{25,9},{2,18},{10... | collective-permute-start | bytes 196616 | tf_op jit(solution)/shard_map/ppermute | solution.py:367
  81.6 6.3 %collective-permute-start.5 = (bf16[256,128]{1,0:T(8,128)(2,1)}, bf16[256,128]{1,0:T(8,128)(2,1)S(1)}, u32[]{:S(2)}, u32[]{:S(2)}) collective-permute-start(bf16[256,128]{1,0:T(8,128)(2,1)} %get-tuple-element.42), channel_id=1, source_target_pairs={{0,24},{8,16},{16,8},{24,0},{1,25},{9,17},{17,9},{25,1},{2,26},{10... | collective-permute-start | bytes 196616 | tf_op jit(solution)/shard_map/ppermute | solution.py:367
  90.3 13.5 %all-to-all-start.2 = ((bf16[8,256,128]{2,1,0:T(8,128)(2,1)}), bf16[8,256,128]{2,1,0:T(8,128)(2,1)S(1)}, u32[]{:S(2)}, u32[]{:S(2)}) async-start(bf16[8,256,128]{2,1,0:T(8,128)(2,1)} %width_back.1), calls=%async_computation.2 | async-start | bytes 1048576 | tf_op jit(solution)/shard_map/all_to_all | solution.py:802
  106.4 13.1 %all-to-all-start.3 = ((bf16[8,256,128]{2,1,0:T(8,128)(2,1)}), bf16[8,256,128]{2,1,0:T(8,128)(2,1)S(1)}, u32[]{:S(2)}, u32[]{:S(2)}) async-start(bf16[8,256,128]{2,1,0:T(8,128)(2,1)} %bitcast.18), calls=%async_computation.3 | async-start | bytes 1048576 | tf_op jit(solution)/shard_map/all_to_all | solution.py:806

commit v4 on v3

--- a/solution.py
+++ b/solution.py
@@ -355,7 +355,7 @@
 
 def partner(me, d, count):
     if count & (count - 1) == 0:
-        return me ^ d
+        return me ^ ((count - d) % count)
     return (me + d) % count
 
 
@@ -370,7 +370,7 @@
 
 def source(me, d, count):
     if count & (count - 1) == 0:
-        return me ^ d
+        return me ^ ((count - d) % count)
     return (me + count - d) % count
 
 

time: 134 us -> 134 us (level)
  waiting for transfers between devices: 15.3 us -> 13.9 us
    ppermute x6, waiting for transfers between devices: 9.7 us -> 8.29 us  [swap_pieces(): moved.append(lax.ppermute(pieces[d], axis, pairs))]
  transfers between devices with their start and end apart: 10 -> 10, of which waited for: 10 -> 8; matrix products, arithmetic and copies ran while one was open for 0% -> 0% of each run, Pallas kernels for 25% -> 25%
where the time goes in v4:
time: 134 us; the launch traced here: 133 us
  Pallas kernels  93.1 us (69%)
  starting transfers between devices  25.8 us (19%)
  waiting for transfers between devices  13.9 us (10%)
    pallas_call x3, Pallas kernels, ahead(): pl.pallas_call(functools.partial(ahead_body, cx, cy, AHEAD_GROUP, first),...  26.4 us
    pallas_call x1, Pallas kernels, encoder(): pl.pallas_call(functools.partial(encoder_body, cx, cy, cap), grid=(blocks...  25.8 us
    pallas_call x1, Pallas kernels, decoder(): pl.pallas_call(functools.partial(decoder_body, cells, group), grid_spec=p...  13.8 us
    pallas_call x1, Pallas kernels, mix(): pl.pallas_call(functools.partial(mix_body, kb, nx, inner), grid=(eb // ea...  9.75 us
    ppermute x6, starting transfers between devices, swap_pieces(): moved.append(lax.ppermute(pieces[d], axis, pairs))  8.77 us
    ppermute x6, waiting for transfers between devices, swap_pieces(): moved.append(lax.ppermute(pieces[d], axis, pairs))  8.29 us
    all_to_all x1, starting transfers between devices, local(): got = swap(payload, 'gy')  5.22 us
    pallas_call x1, Pallas kernels, skip(): pl.pallas_call(functools.partial(skip_body, cap, rows, width, xr), in_spe...  4.85 us
  transfers between devices with their start and end apart: 10, of which 8 were waited for; matrix products, arithmetic and copies ran while one was open for 0% of the time, Pallas kernels for 25%

profile of v4, /device:TPU:0, one launch (start us, length us, event | category | flops | bytes accessed | tf_op | source)
XLA Modules:
  0.0 132.9 jit_solution(4894328693647205390)
XLA Ops:
  0.0 25.8 %encoder.1 = (bf16[8,272,128]{2,1,0:T(8,128)(2,1)}, s32[16]{0:T(128)}) custom-call(s32[16]{0:T(128)} %bitcast.26, s32[16]{0:T(128)} %z_ref.1, f32[3,64]{1,0:T(4,128)} %w_ref.4, f32[3,64]{1,0:T(4,128)} %w_ref.4, f32[1,64]{1,0:T(1,128)} %bitcast.27, bf16[3,16,128]{2,1,0:T(8,128)(2,1)} %bitcast.19, bf16[16,64,128]{2,1,0:T(8,128)(2,1)} %feats_ref.1, ...), custom_call_target="tpu_custom_call" | custom-call | tf_op jit(solution)/shard_map/encoder/pallas_call | solution.py:220
  25.8 5.2 %all-to-all-start = ((bf16[8,272,128]{2,1,0:T(8,128)(2,1)}), bf16[8,272,128]{2,1,0:T(8,128)(2,1)S(1)}, u32[]{:S(2)}, u32[]{:S(2)}) async-start(bf16[8,272,128]{2,1,0:T(8,128)(2,1)} %get-tuple-element.31), calls=%async_computation | async-start | bytes 1114112 | tf_op jit(solution)/shard_map/all_to_all | solution.py:788
  31.0 9.5 %ahead.3.rest_0_ = bf16[16,8192,128]{2,1,0:T(8,128)(2,1)} custom-call(f32[3,64]{1,0:T(4,128)} %w_ref.7, f32[3,64]{1,0:T(4,128)} %w_ref.7, f32[1,64]{1,0:T(1,128)} %bitcast.23, bf16[3,16,128]{2,1,0:T(8,128)(2,1)} %bitcast.20), custom_call_target="tpu_custom_call" | custom-call | tf_op jit(solution)/shard_map/ahead/pallas_call | solution.py:662
  40.5 0.5 all-to-all-done.got_ref
  41.1 0.0 copy-start
  41.1 3.1 %depth_forward.1 = bf16[32,64,128]{2,1,0:T(8,128)(2,1)} custom-call(bf16[8,272,128]{2,1,0:T(8,128)(2,1)S(1)} %all-to-all-done.got_ref, bf16[512,128]{1,0:T(8,128)(2,1)} %constant.27.clone.high_ref, bf16[512,128]{1,0:T(8,128)(2,1)} %constant.28.clone.low_ref), custom_call_target="tpu_custom_call" | custom-call | tf_op jit(solution)/shard_map/depth_forward/pallas_call | solution.py:301
  44.2 3.6 %all-to-all-start.1 = ((bf16[8,256,128]{2,1,0:T(8,128)(2,1)}), bf16[8,256,128]{2,1,0:T(8,128)(2,1)S(1)}, u32[]{:S(2)}, u32[]{:S(2)}) async-start(bf16[8,256,128]{2,1,0:T(8,128)(2,1)} %bitcast.17), calls=%async_computation.1 | async-start | bytes 1048576 | tf_op jit(solution)/shard_map/all_to_all | solution.py:793
  47.8 8.4 %ahead.4.rest_0_ = bf16[16,8192,128]{2,1,0:T(8,128)(2,1)} custom-call(f32[3,64]{1,0:T(4,128)} %w_ref.7, f32[3,64]{1,0:T(4,128)} %w_ref.7, f32[1,64]{1,0:T(1,128)} %bitcast.24, bf16[3,16,128]{2,1,0:T(8,128)(2,1)} %bitcast.21, bf16[16,8192,128]{2,1,0:T(8,128)(2,1)} %ahead.3.rest_0_), custom_call_target="tpu_custom_call", output_to_operand_aliasing={{}: (4, {})} | custom-call | tf_op jit(solution)/shard_map/ahead/pallas_call | solution.py:662
  56.3 0.0 copy-done
  56.3 1.3 all-to-all-done.1.in_ref
  57.5 2.2 %width_forward.1 = (bf16[256,128]{1,0:T(8,128)(2,1)}, bf16[256,128]{1,0:T(8,128)(2,1)}, bf16[256,128]{1,0:T(8,128)(2,1)}, bf16[256,128]{1,0:T(8,128)(2,1)}) custom-call(s32[1]{0:T(128)} %bitcast.3.me_ref, bf16[8,256,128]{2,1,0:T(8,128)(2,1)S(1)} %all-to-all-done.1.in_ref, bf16[256,512]{1,0:T(8,128)(2,1)} %constant.31.clone.high_ref, ...), custom_call_target="tpu_custom_call" | custom-call | tf_op jit(solution)/shard_map/width_forward/pallas_call | solution.py:406
  59.7 3.6 %collective-permute-start = (bf16[256,128]{1,0:T(8,128)(2,1)}, bf16[256,128]{1,0:T(8,128)(2,1)S(1)}, u32[]{:S(2)}, u32[]{:S(2)}) collective-permute-start(bf16[256,128]{1,0:T(8,128)(2,1)} %get-tuple-element.36), channel_id=1, source_target_pairs={{0,24},{8,16},{16,8},{24,0},{1,25},{9,17},{17,9},{25,1},{2,26},{10... | collective-permute-start | bytes 196616 | tf_op jit(solution)/shard_map/ppermute | solution.py:367
  63.3 0.0 collective-permute-start.1
  63.3 0.8 collective-permute-start.2
  64.1 2.4 %collective-permute-done.rest_1_ = bf16[256,128]{1,0:T(8,128)(2,1)S(1)} collective-permute-done((bf16[256,128]{1,0:T(8,128)(2,1)}, bf16[256,128]{1,0:T(8,128)(2,1)S(1)}, u32[]{:S(2)}, u32[]{:S(2)}) %collective-permute-start) | collective-permute-done | bytes 65568 | tf_op jit(solution)/shard_map/ppermute | solution.py:367
  66.5 2.3 %collective-permute-done.1.rest_2_ = bf16[256,128]{1,0:T(8,128)(2,1)S(1)} collective-permute-done((bf16[256,128]{1,0:T(8,128)(2,1)}, bf16[256,128]{1,0:T(8,128)(2,1)S(1)}, u32[]{:S(2)}, u32[]{:S(2)}) %collective-permute-start.1) | collective-permute-done | bytes 65568 | tf_op jit(solution)/shard_map/ppermute | solution.py:367
  68.8 0.0 collective-permute-done.2.rest_3_
  68.8 9.8 %mix.1 = (bf16[256,128]{1,0:T(8,128)(2,1)}, bf16[256,128]{1,0:T(8,128)(2,1)}, bf16[256,128]{1,0:T(8,128)(2,1)}, bf16[256,128]{1,0:T(8,128)(2,1)}) custom-call(s32[1]{0:T(128)} %bitcast.3.me_ref, bf16[256,128]{1,0:T(8,128)(2,1)} %get-tuple-element.35.rest_0_, bf16[256,128]{1,0:T(8,128)(2,1)S(1)} %collective-permute-done.rest_1_, ...), custom_call_target="tpu_custom_call" | custom-call | tf_op jit(solution)/shard_map/mix/pallas_call | solution.py:505
  78.6 2.4 %collective-permute-start.3 = (bf16[256,128]{1,0:T(8,128)(2,1)}, bf16[256,128]{1,0:T(8,128)(2,1)S(1)}, u32[]{:S(2)}, u32[]{:S(2)}) collective-permute-start(bf16[256,128]{1,0:T(8,128)(2,1)} %get-tuple-element.40), channel_id=1, source_target_pairs={{0,24},{8,16},{16,8},{24,0},{1,25},{9,17},{17,9},{25,1},{2,26},{10... | collective-permute-start | bytes 196616 | tf_op jit(solution)/shard_map/ppermute | solution.py:367
  80.9 0.0 collective-permute-start.4
  81.0 2.0 %collective-permute-start.5 = (bf16[256,128]{1,0:T(8,128)(2,1)}, bf16[256,128]{1,0:T(8,128)(2,1)S(1)}, u32[]{:S(2)}, u32[]{:S(2)}) collective-permute-start(bf16[256,128]{1,0:T(8,128)(2,1)} %get-tuple-element.42), channel_id=1, source_target_pairs={{0,8},{8,0},{16,24},{24,16},{1,9},{9,1},{17,25},{25,17},{2,10},{10... | collective-permute-start | bytes 196616 | tf_op jit(solution)/shard_map/ppermute | solution.py:367
  83.0 2.0 %collective-permute-done.3.rest_1_ = bf16[256,128]{1,0:T(8,128)(2,1)S(1)} collective-permute-done((bf16[256,128]{1,0:T(8,128)(2,1)}, bf16[256,128]{1,0:T(8,128)(2,1)S(1)}, u32[]{:S(2)}, u32[]{:S(2)}) %collective-permute-start.3) | collective-permute-done | bytes 65568 | tf_op jit(solution)/shard_map/ppermute | solution.py:367
  85.0 1.6 %collective-permute-done.4.rest_2_ = bf16[256,128]{1,0:T(8,128)(2,1)S(1)} collective-permute-done((bf16[256,128]{1,0:T(8,128)(2,1)}, bf16[256,128]{1,0:T(8,128)(2,1)S(1)}, u32[]{:S(2)}, u32[]{:S(2)}) %collective-permute-start.4) | collective-permute-done | bytes 65568 | tf_op jit(solution)/shard_map/ppermute | solution.py:367
  86.5 0.0 collective-permute-done.5.rest_3_
  86.5 2.3 %width_back.1 = bf16[8,256,128]{2,1,0:T(8,128)(2,1)} custom-call(s32[1]{0:T(128)} %bitcast.3.me_ref, bf16[256,128]{1,0:T(8,128)(2,1)} %get-tuple-element.39.rest_0_, bf16[256,128]{1,0:T(8,128)(2,1)S(1)} %collective-permute-done.3.rest_1_, bf16[256,128]{1,0:T(8,128)(2,1)S(1)} %collective-permute-done.4.rest_2_, ...), custom_call_target="tpu_custom_call" | custom-call | tf_op jit(solution)/shard_map/width_back/pallas_call | solution.py:562
  88.9 4.7 %all-to-all-start.2 = ((bf16[8,256,128]{2,1,0:T(8,128)(2,1)}), bf16[8,256,128]{2,1,0:T(8,128)(2,1)S(1)}, u32[]{:S(2)}, u32[]{:S(2)}) async-start(bf16[8,256,128]{2,1,0:T(8,128)(2,1)} %width_back.1), calls=%async_computation.2 | async-start | bytes 1048576 | tf_op jit(solution)/shard_map/all_to_all | solution.py:802
  93.6 2.3 %spread.1 = (bf16[64,64,128]{2,1,0:T(8,128)(2,1)}, f32[64,128]{1,0:T(8,128)}) custom-call(bf16[64,64]{1,0:T(8,128)(2,1)} %out_w_ref.3, f32[1,64]{1,0:T(1,128)} %bitcast.29), custom_call_target="tpu_custom_call" | custom-call | tf_op jit(solution)/shard_map/spread/pallas_call | solution.py:621
  95.9 4.8 %skip.1 = (f32[32,64,128]{2,1,0:T(8,128)}, bf16[256,256]{1,0:T(8,128)(2,1)}, bf16[256,256]{1,0:T(8,128)(2,1)}) custom-call(bf16[8,272,128]{2,1,0:T(8,128)(2,1)} %copy-done, f32[64,64]{1,0:T(8,128)} %weight_ref.1, f32[1,64]{1,0:T(1,128)} %bitcast.28, bf16[256,128]{1,0:T(8,128)(2,1)} %constant.29.clone.high_ref, bf16[256,128]{1,0:T(8,128)(2,1)} %constant.30.clone.low_ref), custom_call_target="tpu_custom_call" | custom-call | tf_op jit(solution)/shard_map/skip/pallas_call | solution.py:341
  100.7 2.6 %all-to-all-done.2.in_ref = bf16[8,256,128]{2,1,0:T(8,128)(2,1)S(1)} async-done(((bf16[8,256,128]{2,1,0:T(8,128)(2,1)}), bf16[8,256,128]{2,1,0:T(8,128)(2,1)S(1)}, u32[]{:S(2)}, u32[]{:S(2)}) %all-to-all-start.2) | async-done | bytes 524320 | tf_op jit(solution)/shard_map/all_to_all | solution.py:802
  103.3 2.6 %latent.1 = bf16[32,64,128]{2,1,0:T(8,128)(2,1)} custom-call(bf16[8,256,128]{2,1,0:T(8,128)(2,1)S(1)} %all-to-all-done.2.in_ref, f32[32,64,128]{2,1,0:T(8,128)} %get-tuple-element.49.skip_ref, bf16[256,256]{1,0:T(8,128)(2,1)} %get-tuple-element.50.high_ref, bf16[256,256]{1,0:T(8,128)(2,1)} %get-tuple-element.51.low_ref), custom_call_target="tpu_custom_call" | custom-call | tf_op jit(solution)/shard_map/latent/pallas_call | solution.py:595
  105.9 3.5 %all-to-all-start.3 = ((bf16[8,256,128]{2,1,0:T(8,128)(2,1)}), bf16[8,256,128]{2,1,0:T(8,128)(2,1)S(1)}, u32[]{:S(2)}, u32[]{:S(2)}) async-start(bf16[8,256,128]{2,1,0:T(8,128)(2,1)} %bitcast.18), calls=%async_computation.3 | async-start | bytes 1048576 | tf_op jit(solution)/shard_map/all_to_all | solution.py:806
  109.4 8.4 %ahead.5.rest_1_ = bf16[16,8192,128]{2,1,0:T(8,128)(2,1)} custom-call(f32[3,64]{1,0:T(4,128)} %w_ref.7, f32[3,64]{1,0:T(4,128)} %w_ref.7, f32[1,64]{1,0:T(1,128)} %bitcast.25, bf16[3,16,128]{2,1,0:T(8,128)(2,1)} %bitcast.22, bf16[16,8192,128]{2,1,0:T(8,128)(2,1)} %ahead.4.rest_0_), custom_call_target="tpu_custom_call", output_to_operand_aliasing={{}: (4, {})} | custom-call | tf_op jit(solution)/shard_map/ahead/pallas_call | solution.py:662
  117.8 1.2 all-to-all-done.3
  119.1 13.8 %decoder.1 = f32[16,128]{1,0:T(8,128)} custom-call(s32[16]{0:T(128)} %get-tuple-element.30.slot_ref, bf16[32,64,128]{2,1,0:T(8,128)(2,1)S(1)} %bitcast.15, bf16[16,8192,128]{2,1,0:T(8,128)(2,1)} %ahead.5.rest_1_, bf16[64,64,128]{2,1,0:T(8,128)(2,1)} %get-tuple-element.53.rest_2_, f32[64,128]{1,0:T(8,128)} %get-tuple-element.54.rest_3_), custom_call_target="tpu_custom_call" | custom-call | tf_op jit(solution)/shard_map/decoder/pallas_call | solution.py:715
Async XLA Ops:
  25.8 15.3 %all-to-all-start = ((bf16[8,272,128]{2,1,0:T(8,128)(2,1)}), bf16[8,272,128]{2,1,0:T(8,128)(2,1)S(1)}, u32[]{:S(2)}, u32[]{:S(2)}) async-start(bf16[8,272,128]{2,1,0:T(8,128)(2,1)} %get-tuple-element.31), calls=%async_computation | async-start | bytes 1114112 | tf_op jit(solution)/shard_map/all_to_all | solution.py:788
  41.1 15.2 %copy-start = (bf16[8,272,128]{2,1,0:T(8,128)(2,1)}, bf16[8,272,128]{2,1,0:T(8,128)(2,1)S(1)}, u32[]{:S(2)}) copy-start(bf16[8,272,128]{2,1,0:T(8,128)(2,1)S(1)} %all-to-all-done.got_ref) | copy-start | bytes 1671172
  44.2 13.4 %all-to-all-start.1 = ((bf16[8,256,128]{2,1,0:T(8,128)(2,1)}), bf16[8,256,128]{2,1,0:T(8,128)(2,1)S(1)}, u32[]{:S(2)}, u32[]{:S(2)}) async-start(bf16[8,256,128]{2,1,0:T(8,128)(2,1)} %bitcast.17), calls=%async_computation.1 | async-start | bytes 1048576 | tf_op jit(solution)/shard_map/all_to_all | solution.py:793
  59.7 6.8 %collective-permute-start = (bf16[256,128]{1,0:T(8,128)(2,1)}, bf16[256,128]{1,0:T(8,128)(2,1)S(1)}, u32[]{:S(2)}, u32[]{:S(2)}) collective-permute-start(bf16[256,128]{1,0:T(8,128)(2,1)} %get-tuple-element.36), channel_id=1, source_target_pairs={{0,24},{8,16},{16,8},{24,0},{1,25},{9,17},{17,9},{25,1},{2,26},{10... | collective-permute-start | bytes 196616 | tf_op jit(solution)/shard_map/ppermute | solution.py:367
  63.3 5.5 %collective-permute-start.1 = (bf16[256,128]{1,0:T(8,128)(2,1)}, bf16[256,128]{1,0:T(8,128)(2,1)S(1)}, u32[]{:S(2)}, u32[]{:S(2)}) collective-permute-start(bf16[256,128]{1,0:T(8,128)(2,1)} %get-tuple-element.37), channel_id=1, source_target_pairs={{0,16},{8,24},{16,0},{24,8},{1,17},{9,25},{17,1},{25,9},{2,18},{10... | collective-permute-start | bytes 196616 | tf_op jit(solution)/shard_map/ppermute | solution.py:367
  63.3 5.5 %collective-permute-start.2 = (bf16[256,128]{1,0:T(8,128)(2,1)}, bf16[256,128]{1,0:T(8,128)(2,1)S(1)}, u32[]{:S(2)}, u32[]{:S(2)}) collective-permute-start(bf16[256,128]{1,0:T(8,128)(2,1)} %get-tuple-element.38), channel_id=1, source_target_pairs={{0,8},{8,0},{16,24},{24,16},{1,9},{9,1},{17,25},{25,17},{2,10},{10... | collective-permute-start | bytes 196616 | tf_op jit(solution)/shard_map/ppermute | solution.py:367
  78.6 6.4 %collective-permute-start.3 = (bf16[256,128]{1,0:T(8,128)(2,1)}, bf16[256,128]{1,0:T(8,128)(2,1)S(1)}, u32[]{:S(2)}, u32[]{:S(2)}) collective-permute-start(bf16[256,128]{1,0:T(8,128)(2,1)} %get-tuple-element.40), channel_id=1, source_target_pairs={{0,24},{8,16},{16,8},{24,0},{1,25},{9,17},{17,9},{25,1},{2,26},{10... | collective-permute-start | bytes 196616 | tf_op jit(solution)/shard_map/ppermute | solution.py:367
  80.9 5.6 %collective-permute-start.4 = (bf16[256,128]{1,0:T(8,128)(2,1)}, bf16[256,128]{1,0:T(8,128)(2,1)S(1)}, u32[]{:S(2)}, u32[]{:S(2)}) collective-permute-start(bf16[256,128]{1,0:T(8,128)(2,1)} %get-tuple-element.41), channel_id=1, source_target_pairs={{0,16},{8,24},{16,0},{24,8},{1,17},{9,25},{17,1},{25,9},{2,18},{10... | collective-permute-start | bytes 196616 | tf_op jit(solution)/shard_map/ppermute | solution.py:367
  81.0 5.6 %collective-permute-start.5 = (bf16[256,128]{1,0:T(8,128)(2,1)}, bf16[256,128]{1,0:T(8,128)(2,1)S(1)}, u32[]{:S(2)}, u32[]{:S(2)}) collective-permute-start(bf16[256,128]{1,0:T(8,128)(2,1)} %get-tuple-element.42), channel_id=1, source_target_pairs={{0,8},{8,0},{16,24},{24,16},{1,9},{9,1},{17,25},{25,17},{2,10},{10... | collective-permute-start | bytes 196616 | tf_op jit(solution)/shard_map/ppermute | solution.py:367
  88.9 14.4 %all-to-all-start.2 = ((bf16[8,256,128]{2,1,0:T(8,128)(2,1)}), bf16[8,256,128]{2,1,0:T(8,128)(2,1)S(1)}, u32[]{:S(2)}, u32[]{:S(2)}) async-start(bf16[8,256,128]{2,1,0:T(8,128)(2,1)} %width_back.1), calls=%async_computation.2 | async-start | bytes 1048576 | tf_op jit(solution)/shard_map/all_to_all | solution.py:802
  105.9 13.1 %all-to-all-start.3 = ((bf16[8,256,128]{2,1,0:T(8,128)(2,1)}), bf16[8,256,128]{2,1,0:T(8,128)(2,1)S(1)}, u32[]{:S(2)}, u32[]{:S(2)}) async-start(bf16[8,256,128]{2,1,0:T(8,128)(2,1)} %bitcast.18), calls=%async_computation.3 | async-start | bytes 1048576 | tf_op jit(solution)/shard_map/all_to_all | solution.py:806
